TPU v7x, 1024 devices: a whole 4x8x16 slice. The times are simulated.
1024 devices in a mesh: grp: 16 (over x_hi, y), dev: 64 (over z, x_lo, core).
Axes of the slice: x: 4 (x_hi: 2, x_lo: 2; x = x_hi * 2 + x_lo), y: 8, z: 16, core: 2. Of those that a mesh axis runs over, the one named last changes fastest.
Arguments:
- state: float32 [2, 8, 4194304], P(None, None, ('grp', 'dev')), may hold values from -6 to 6
- gates: float32 [2, 4, 2, 128, 128], replicated, may hold values from -0.375 to 0.375
- local_perm: int32 [2, 12], replicated, may hold values from 0 to 11, each once within a row
Outputs:
- final_state: float32 [2, 8, 4194304], P(None, None, ('grp', 'dev'))
Inputs may be any that keep to these rules, and one draw needn't show every extreme that they name: Each row of local_perm names each of the 12 local qubits once.
All inputs are finite; a program needn't handle non-finite values.
Results may differ from a plain program's by a relative error of at most 0.0001.
Values sent between devices are 32-bit elements; how exact they have to be, the bound alone decides.
No kernel may reach another device: no remote copies, remote signals or barrier semaphores. Data moves between devices by JAX's collectives and lax.ppermute only.
A program may use at most 32 MiB of HBM per device.

v0:
```python
import functools

import jax
import jax.numpy as jnp
from jax import lax
from jax.experimental import pallas as pl
from jax.experimental.pallas import tpu as pltpu
from jax.sharding import PartitionSpec as P

CYCLES = 2
LANE_BITS = 7
TILE_BITS = 5
TILES = 1 << TILE_BITS
SUBLANES = 8
LANES = 1 << LANE_BITS
WIDE = 2 * LANES


def lane_iota(shape):
    return lax.broadcasted_iota(jnp.int32, shape, len(shape) - 1)


def sublane_iota(shape):
    return lax.broadcasted_iota(jnp.int32, shape, len(shape) - 2)


def halves(array):
    high = array.astype(jnp.bfloat16)
    return high, (array - high.astype(jnp.float32)).astype(jnp.bfloat16)


def product(left, right, contract):
    left_high, left_low = halves(left)
    right_high, right_low = halves(right)
    dims = (contract, ((), ()))
    dot = functools.partial(lax.dot_general, dimension_numbers=dims, preferred_element_type=jnp.float32)
    return dot(left_high, right_high) + (dot(left_high, right_low) + dot(left_low, right_high))


def swap_sublane_lane(tiles, sublane_bit, lane_bit):
    step, hop = 1 << sublane_bit, 1 << lane_bit
    one_tile = (1, SUBLANES, LANES)
    in_sublane = sublane_iota(one_tile) >> sublane_bit & 1
    in_lane = lane_iota(one_tile) >> lane_bit & 1
    flipped = jnp.where(in_sublane == 0, pltpu.roll(tiles, SUBLANES - step, 1), pltpu.roll(tiles, step, 1))
    if 2 * hop == LANES:
        flipped = pltpu.roll(flipped, hop, 2)
    else:
        flipped = jnp.where(in_lane == 0, pltpu.roll(flipped, LANES - hop, 2), pltpu.roll(flipped, hop, 2))
    return jnp.where(in_sublane == in_lane, tiles, flipped)


def shuffle(tiles):
    tiles = swap_sublane_lane(tiles, 0, 5)
    tiles = swap_sublane_lane(tiles, 1, 6)
    pairs = tiles.reshape(-1, 2, SUBLANES, LANES)
    even, odd = pairs[:, 0], pairs[:, 1]
    lower = sublane_iota((1, SUBLANES, LANES)) < SUBLANES // 2
    new_even = jnp.where(lower, even, pltpu.roll(odd, SUBLANES // 2, 1))
    new_odd = jnp.where(lower, pltpu.roll(even, SUBLANES // 2, 1), odd)
    return jnp.stack([new_even, new_odd], axis=1).reshape(tiles.shape)


def wide_gate(real, imag):
    return jnp.concatenate(
        [jnp.concatenate([real, -imag], axis=1), jnp.concatenate([imag, real], axis=1)], axis=0
    )


def take_lanes(array, index):
    rows = [
        jnp.take_along_axis(array[r : r + SUBLANES], index, axis=1) for r in range(0, array.shape[0], SUBLANES)
    ]
    return jnp.concatenate(rows, axis=0)


def apply_rows(tiles, gate):
    parts = tiles.reshape(2, TILES * SUBLANES, LANES)
    return product(jnp.concatenate([parts[0], parts[1]], axis=1), gate, ((1,), (1,)))


def apply_columns(tiles, gate):
    pairs = shuffle(tiles).reshape(TILES, 2, SUBLANES, LANES)
    columns = jnp.concatenate(
        [pairs[:, 0].reshape(WIDE, LANES), pairs[:, 1].reshape(WIDE, LANES)], axis=1
    )
    out = product(gate, columns, ((1,), (0,)))
    back = jnp.stack(
        [out[:, :LANES].reshape(TILES, SUBLANES, LANES), out[:, LANES:].reshape(TILES, SUBLANES, LANES)], axis=1
    )
    return shuffle(back.reshape(2 * TILES, SUBLANES, LANES))


def received_gate(gate_ref):
    real, imag = gate_ref[0], gate_ref[1]
    lane = lane_iota((SUBLANES, LANES))
    part = lane_iota((1, LANES)) >> 1 & 1
    blocks = []
    for half in range(2):
        index = half * (LANES // 2) + ((lane >> 2) << 1) + (lane & 1)
        real_half, imag_half = take_lanes(real, index), take_lanes(imag, index)
        blocks.append(
            jnp.concatenate(
                [jnp.where(part == 0, real_half, -imag_half), jnp.where(part == 0, imag_half, real_half)], axis=0
            )
        )
    return jnp.concatenate(blocks, axis=1)


def plan(perm_ref, cycle):
    one = jnp.int32(1)
    source = [perm_ref[cycle, b] for b in range(LANE_BITS + TILE_BITS)]
    crosses = [
        jnp.where(source[b] >= LANE_BITS, 1, 0) if b < LANE_BITS else jnp.where(source[b] < LANE_BITS, 1, 0)
        for b in range(LANE_BITS + TILE_BITS)
    ]
    count = sum(crosses[1:LANE_BITS], crosses[0])
    place = []
    for first, last in ((0, LANE_BITS), (LANE_BITS, LANE_BITS + TILE_BITS)):
        ahead = jnp.int32(0)
        for b in range(first, last):
            place.append(jnp.where(crosses[b] == 1, ahead, count + (b - first) - ahead))
            ahead = ahead + crosses[b]
    tile_from, tile_to = [], []
    for at in range(TILE_BITS):
        origin, target = jnp.int32(0), jnp.int32(0)
        for b in range(LANE_BITS + TILE_BITS):
            is_tile_source = source[b] >= LANE_BITS
            bit = lax.shift_left(one, jnp.maximum(source[b] - LANE_BITS, 0))
            origin = origin + jnp.where(jnp.logical_and(is_tile_source, place[b] == at), bit, 0)
            if b >= LANE_BITS:
                target = target + jnp.where(place[b] == at, 1 << (b - LANE_BITS), 0)
        tile_from.append(origin)
        tile_to.append(target)
    lane = lane_iota((SUBLANES, LANES))
    lane_from = jnp.zeros((SUBLANES, LANES), jnp.int32)
    lane_to = jnp.zeros((SUBLANES, LANES), jnp.int32)
    for b in range(LANE_BITS + TILE_BITS):
        bit = lax.shift_right_logical(lane, jnp.full((SUBLANES, LANES), place[b])) & 1
        shift = jnp.full((SUBLANES, LANES), jnp.where(source[b] < LANE_BITS, source[b], 0))
        keep = jnp.where(source[b] < LANE_BITS, 1, 0)
        lane_from = lane_from + lax.shift_left(bit * keep, shift)
        if b < LANE_BITS:
            lane_to = lane_to + (bit << b)
    return count, tile_from, tile_to, lane_from, lane_to


def combine(basis, value):
    total = jnp.int32(0)
    for bit in range(TILE_BITS):
        if value >> bit & 1:
            total = total + basis[bit]
    return total


def permute(load, store, scalars):
    count, tile_from, tile_to, lane_from, _ = scalars
    lane = lane_iota((SUBLANES, LANES))
    for part in range(2):
        tiles = [
            jnp.take_along_axis(load(part, combine(tile_from, at)), lane_from, axis=1) for at in range(TILES)
        ]
        for j in range(TILE_BITS):
            hop = 1 << j
            idle = jnp.full((SUBLANES, LANES), jnp.where(count > j, 0, 1)) == 1
            in_lane = lane >> j & 1
            keep_even = jnp.logical_or(in_lane == 0, idle)
            keep_odd = jnp.logical_or(in_lane == 1, idle)
            for at in range(TILES):
                if at & hop:
                    continue
                even, odd = tiles[at], tiles[at + hop]
                tiles[at] = jnp.where(keep_even, even, pltpu.roll(odd, hop, 1))
                tiles[at + hop] = jnp.where(keep_odd, odd, pltpu.roll(even, LANES - hop, 1))
        for at in range(TILES):
            store(part, combine(tile_to, at), tiles[at])


def local_gates(cycle, load, perm_ref, own_ref, gates, scratch, kept_ref, sent_ref):
    scalars = plan(perm_ref, cycle)

    def store(part, tile, value):
        scratch[part, tile] = value

    permute(load, store, scalars)
    lane_to = scalars[-1]
    first = wide_gate(take_lanes(gates[0, 0], lane_to), take_lanes(gates[0, 1], lane_to))
    out = apply_rows(scratch[...].reshape(2 * TILES, SUBLANES, LANES), first)
    tiles = jnp.concatenate(
        [out[:, :LANES].reshape(TILES, SUBLANES, LANES), out[:, LANES:].reshape(TILES, SUBLANES, LANES)], axis=0
    )
    tiles = apply_columns(tiles, wide_gate(gates[1, 0], gates[1, 1]))
    real, imag = gates[2, 0], gates[2, 1]
    cut = LANES // 2
    last = jnp.concatenate(
        [
            wide_gate(real, imag)[at : at + cut]
            for at in (0, LANES, cut, LANES + cut)
        ],
        axis=0,
    )
    out = apply_rows(tiles, last)
    kept_ref[:, 0] = out[:, :LANES].reshape(TILES, SUBLANES, LANES)
    kept_ref[:, 1] = out[:, LANES:].reshape(TILES, SUBLANES, LANES)
    sent_ref[...] = kept_ref[pl.ds((1 - own_ref[0]) * (TILES // 2), TILES // 2)]


def first_kernel(perm_ref, own_ref, state_ref, gates_ref, kept_ref, sent_ref, scratch):
    def load(part, tile):
        return state_ref[part, :, pl.ds(pl.multiple_of(tile * LANES, LANES), LANES)]

    local_gates(0, load, perm_ref, own_ref, gates_ref.at[0], scratch, kept_ref, sent_ref)


def middle_kernel(perm_ref, own_ref, tiles_ref, gates_ref, kept_ref, sent_ref, before, scratch):
    before[...] = apply_columns(tiles_ref[...], received_gate(gates_ref.at[0, 3])).reshape(before.shape)

    def load(part, tile):
        return before[part, tile]

    local_gates(1, load, perm_ref, own_ref, gates_ref.at[1], scratch, kept_ref, sent_ref)


def last_kernel(tiles_ref, gates_ref, out_ref):
    tiles = apply_columns(tiles_ref[...], received_gate(gates_ref.at[1, 3])).reshape(2, TILES, SUBLANES, LANES)
    for tile in range(TILES):
        out_ref[:, :, tile * LANES : (tile + 1) * LANES] = tiles[:, tile]


SMEM = pl.BlockSpec(memory_space=pltpu.SMEM)
VMEM = pl.BlockSpec(memory_space=pltpu.VMEM)
TILE_SHAPE = (2 * TILES, SUBLANES, LANES)
SCRATCH = pltpu.VMEM((2, TILES, SUBLANES, LANES), jnp.float32)
TO_SEND = (
    jax.ShapeDtypeStruct((TILES, 2, SUBLANES, LANES), jnp.float32),
    jax.ShapeDtypeStruct((TILES // 2, 2, SUBLANES, LANES), jnp.float32),
)


def exchange(kept, sent, own, which):
    pairs = [(i, i ^ 1 << which) for i in range(lax.axis_size("grp"))]
    received = lax.ppermute(sent, "grp", pairs)
    joined = lax.dynamic_update_slice(kept, received, ((1 - own) * (TILES // 2), 0, 0, 0))
    return lax.all_to_all(joined.reshape(TILE_SHAPE), "dev", split_axis=0, concat_axis=0, tiled=True)


def on_device(state, gates, local_perm):
    grp = lax.axis_index("grp")
    owns = [grp >> cycle & 1 for cycle in range(CYCLES)]
    kept, sent = pl.pallas_call(
        first_kernel,
        out_shape=TO_SEND,
        in_specs=[SMEM, SMEM, VMEM, VMEM],
        out_specs=(VMEM, VMEM),
        scratch_shapes=[SCRATCH],
    )(local_perm, owns[0].reshape(1), state, gates)
    tiles = exchange(kept, sent, owns[0], 0)
    kept, sent = pl.pallas_call(
        middle_kernel,
        out_shape=TO_SEND,
        in_specs=[SMEM, SMEM, VMEM, VMEM],
        out_specs=(VMEM, VMEM),
        scratch_shapes=[SCRATCH, SCRATCH],
    )(local_perm, owns[1].reshape(1), tiles, gates)
    tiles = exchange(kept, sent, owns[1], 1)
    return pl.pallas_call(
        last_kernel,
        out_shape=jax.ShapeDtypeStruct(state.shape, jnp.float32),
        in_specs=[VMEM, VMEM],
        out_specs=VMEM,
    )(tiles, gates)


def solution(mesh):
    placed = (P(None, None, ("grp", "dev")), P(), P())
    return jax.shard_map(
        on_device,
        mesh=mesh,
        in_specs=placed,
        out_specs=P(None, None, ("grp", "dev")),
        check_vma=False,
    )
```

profile of v0, /device:TPU:1, one launch (start us, length us, event | category | flops | bytes accessed | tf_op | source)
XLA Modules:
  0.0 104.0 jit_solution(7305374734521364982)
XLA Ops:
  0.0 4.1 %shard_map.37 = (f32[32,2,8,128]{3,2,1,0:T(8,128)}, f32[16,2,8,128]{3,2,1,0:T(8,128)}) custom-call(s32[2,12]{1,0:T(2,128)} %perm_ref.3, s32[1]{0:T(128)} %bitcast.1.own_ref, f32[2,8,4096]{2,1,0:T(8,128)} %state_ref.1, f32[2,4,2,128,128]{4,3,2,1,0:T(8,128)} %gates_ref.5), custom_call_target="tpu_custom_call" | custom-call | tf_op jit(solution)/shard_map/pallas_call | solution.py:250
  4.1 4.0 %collective-permute-start = (f32[16,2,8,128]{3,2,1,0:T(8,128)}, f32[16,2,8,128]{3,2,1,0:T(8,128)S(1)}, u32[]{:S(2)}, u32[]{:S(2)}) collective-permute-start(f32[16,2,8,128]{3,2,1,0:T(8,128)} %get-tuple-element.10), channel_id=1, source_target_pairs={{0,64},{64,0},{128,192},{192,128},{256,320},{320,256},{384,448},{4... | collective-permute-start | bytes 393224 | tf_op jit(solution)/shard_map/ppermute | solution.py:242
  8.1 2.5 %collective-permute-done = f32[16,2,8,128]{3,2,1,0:T(8,128)S(1)} collective-permute-done((f32[16,2,8,128]{3,2,1,0:T(8,128)}, f32[16,2,8,128]{3,2,1,0:T(8,128)S(1)}, u32[]{:S(2)}, u32[]{:S(2)}) %collective-permute-start) | collective-permute-done | bytes 131104 | tf_op jit(solution)/shard_map/ppermute | solution.py:242
  10.7 0.7 constant_dynamic-update-slice_fusion.1
  11.3 22.5 %all-to-all-start = ((f32[64,8,128]{2,1,0:T(8,128)}), f32[64,8,128]{2,1,0:T(8,128)S(1)}, u32[]{:S(2)}, u32[]{:S(2)}) async-start(f32[64,8,128]{2,1,0:T(8,128)} %bitcast.5), calls=%async_computation | async-start | bytes 524288 | tf_op jit(solution)/shard_map/all_to_all | solution.py:244
  33.8 22.3 %all-to-all-done.tiles_ref = f32[64,8,128]{2,1,0:T(8,128)S(1)} async-done(((f32[64,8,128]{2,1,0:T(8,128)}), f32[64,8,128]{2,1,0:T(8,128)S(1)}, u32[]{:S(2)}, u32[]{:S(2)}) %all-to-all-start) | async-done | bytes 262176 | tf_op jit(solution)/shard_map/all_to_all | solution.py:244
  56.1 0.0 copy-start
  56.1 0.7 copy-done
  56.8 4.9 %shard_map.38 = (f32[32,2,8,128]{3,2,1,0:T(8,128)}, f32[16,2,8,128]{3,2,1,0:T(8,128)}) custom-call(s32[2,12]{1,0:T(2,128)} %perm_ref.3, s32[1]{0:T(128)} %bitcast.own_ref, f32[64,8,128]{2,1,0:T(8,128)} %copy-done, f32[2,4,2,128,128]{4,3,2,1,0:T(8,128)} %gates_ref.5), custom_call_target="tpu_custom_call" | custom-call | tf_op jit(solution)/shard_map/pallas_call | solution.py:258
  61.7 4.2 %collective-permute-start.1 = (f32[16,2,8,128]{3,2,1,0:T(8,128)}, f32[16,2,8,128]{3,2,1,0:T(8,128)S(1)}, u32[]{:S(2)}, u32[]{:S(2)}) collective-permute-start(f32[16,2,8,128]{3,2,1,0:T(8,128)} %get-tuple-element.12), channel_id=1, source_target_pairs={{0,128},{64,192},{128,0},{192,64},{256,384},{320,448},{384,256},{4... | collective-permute-start | bytes 393224 | tf_op jit(solution)/shard_map/ppermute | solution.py:242
  65.9 6.1 %collective-permute-done.1 = f32[16,2,8,128]{3,2,1,0:T(8,128)S(1)} collective-permute-done((f32[16,2,8,128]{3,2,1,0:T(8,128)}, f32[16,2,8,128]{3,2,1,0:T(8,128)S(1)}, u32[]{:S(2)}, u32[]{:S(2)}) %collective-permute-start.1) | collective-permute-done | bytes 131104 | tf_op jit(solution)/shard_map/ppermute | solution.py:242
  72.0 0.7 constant_dynamic-update-slice_fusion
  72.7 28.6 %all_to_all.10.tiles_ref = f32[64,8,128]{2,1,0:T(8,128)} all-to-all(f32[64,8,128]{2,1,0:T(8,128)} %bitcast.4), channel_id=1, replica_groups=mesh['grp'=16,'dev'=64] {'dev'}, dimensions={0} | all-to-all | bytes 524288 | tf_op jit(solution)/shard_map/all_to_all | solution.py:244
  101.2 2.8 %shard_map.39 = f32[2,8,4096]{2,1,0:T(8,128)} custom-call(f32[64,8,128]{2,1,0:T(8,128)} %all_to_all.10.tiles_ref, f32[2,4,2,128,128]{4,3,2,1,0:T(8,128)} %gates_ref.5), custom_call_target="tpu_custom_call" | custom-call | tf_op jit(solution)/shard_map/pallas_call | solution.py:266
Async XLA Ops:
  4.1 6.6 %collective-permute-start = (f32[16,2,8,128]{3,2,1,0:T(8,128)}, f32[16,2,8,128]{3,2,1,0:T(8,128)S(1)}, u32[]{:S(2)}, u32[]{:S(2)}) collective-permute-start(f32[16,2,8,128]{3,2,1,0:T(8,128)} %get-tuple-element.10), channel_id=1, source_target_pairs={{0,64},{64,0},{128,192},{192,128},{256,320},{320,256},{384,448},{4... | collective-permute-start | bytes 393224 | tf_op jit(solution)/shard_map/ppermute | solution.py:242
  11.3 44.8 %all-to-all-start = ((f32[64,8,128]{2,1,0:T(8,128)}), f32[64,8,128]{2,1,0:T(8,128)S(1)}, u32[]{:S(2)}, u32[]{:S(2)}) async-start(f32[64,8,128]{2,1,0:T(8,128)} %bitcast.5), calls=%async_computation | async-start | bytes 524288 | tf_op jit(solution)/shard_map/all_to_all | solution.py:244
  56.1 0.7 copy-start
  61.7 10.3 %collective-permute-start.1 = (f32[16,2,8,128]{3,2,1,0:T(8,128)}, f32[16,2,8,128]{3,2,1,0:T(8,128)S(1)}, u32[]{:S(2)}, u32[]{:S(2)}) collective-permute-start(f32[16,2,8,128]{3,2,1,0:T(8,128)} %get-tuple-element.12), channel_id=1, source_target_pairs={{0,128},{64,192},{128,0},{192,64},{256,384},{320,448},{384,256},{4... | collective-permute-start | bytes 393224 | tf_op jit(solution)/shard_map/ppermute | solution.py:242
where the time goes:
time: 104 us
  waiting for transfers between devices  30.9 us (30%)
  starting transfers between devices  30.7 us (30%)
  blocking collectives  28.6 us (28%)
  Pallas kernels  11.8 us (11%)
  local copies, waits for them, and re-layouts  2.02 us (2%)
    all_to_all x1, blocking collectives, exchange(): lax.all_to_all(joined.reshape(TILE_SHAPE), 'dev', split_axis=0, concat_ax...  28.6 us
    all_to_all x1, starting transfers between devices, exchange(): lax.all_to_all(joined.reshape(TILE_SHAPE), 'dev', split_axis=0, concat_ax...  22.5 us
    all_to_all x1, waiting for transfers between devices, exchange(): lax.all_to_all(joined.reshape(TILE_SHAPE), 'dev', split_axis=0, concat_ax...  22.3 us
    ppermute x2, waiting for transfers between devices, exchange(): received = lax.ppermute(sent, 'grp', pairs)  8.61 us
    ppermute x2, starting transfers between devices, exchange(): received = lax.ppermute(sent, 'grp', pairs)  8.21 us
    pallas_call x1, Pallas kernels, on_device(): pl.pallas_call(middle_kernel, out_shape=TO_SEND, in_specs=[SMEM, SMEM, VM...  4.9 us
    pallas_call x1, Pallas kernels, on_device(): pl.pallas_call(first_kernel, out_shape=TO_SEND, in_specs=[SMEM, SMEM, VME...  4.1 us
    pallas_call x1, Pallas kernels, on_device(): pl.pallas_call(last_kernel, out_shape=jax.ShapeDtypeStruct(state.shape, j...  2.82 us
  transfers between devices with their start and end apart: 3, of which 3 were waited for; matrix products, arithmetic and copies ran while one was open for 0% of the time, Pallas kernels for 0%

commit v1 on v0

--- a/solution.py
+++ b/solution.py
@@ -5,7 +5,7 @@
 from jax import lax
 from jax.experimental import pallas as pl
 from jax.experimental.pallas import tpu as pltpu
-from jax.sharding import PartitionSpec as P
+from jax.sharding import Mesh, PartitionSpec as P
 
 CYCLES = 2
 LANE_BITS = 7
@@ -50,15 +50,19 @@
     return jnp.where(in_sublane == in_lane, tiles, flipped)
 
 
+def swap_sublane_tile(low, high, sublane_bit):
+    step = 1 << sublane_bit
+    clear = sublane_iota((1, SUBLANES, LANES)) >> sublane_bit & 1 == 0
+    new_low = jnp.where(clear, low, pltpu.roll(high, step, 1))
+    new_high = jnp.where(clear, pltpu.roll(low, SUBLANES - step, 1), high)
+    return new_low, new_high
+
+
 def shuffle(tiles):
     tiles = swap_sublane_lane(tiles, 0, 5)
     tiles = swap_sublane_lane(tiles, 1, 6)
     pairs = tiles.reshape(-1, 2, SUBLANES, LANES)
-    even, odd = pairs[:, 0], pairs[:, 1]
-    lower = sublane_iota((1, SUBLANES, LANES)) < SUBLANES // 2
-    new_even = jnp.where(lower, even, pltpu.roll(odd, SUBLANES // 2, 1))
-    new_odd = jnp.where(lower, pltpu.roll(even, SUBLANES // 2, 1), odd)
-    return jnp.stack([new_even, new_odd], axis=1).reshape(tiles.shape)
+    return jnp.stack(swap_sublane_tile(pairs[:, 0], pairs[:, 1], 2), axis=1).reshape(tiles.shape)
 
 
 def wide_gate(real, imag):
@@ -91,13 +95,12 @@
     return shuffle(back.reshape(2 * TILES, SUBLANES, LANES))
 
 
-def received_gate(gate_ref):
-    real, imag = gate_ref[0], gate_ref[1]
+def interleaved_gate(real, imag, index_of, part_bit):
     lane = lane_iota((SUBLANES, LANES))
-    part = lane_iota((1, LANES)) >> 1 & 1
+    part = lane_iota((1, LANES)) >> part_bit & 1
     blocks = []
     for half in range(2):
-        index = half * (LANES // 2) + ((lane >> 2) << 1) + (lane & 1)
+        index = index_of(half, lane)
         real_half, imag_half = take_lanes(real, index), take_lanes(imag, index)
         blocks.append(
             jnp.concatenate(
@@ -105,6 +108,29 @@
             )
         )
     return jnp.concatenate(blocks, axis=1)
+
+
+def middle_gate(gate_ref):
+    def index_of(half, lane):
+        return half * (LANES // 2) + ((lane >> 2) << 1) + (lane & 1)
+
+    return interleaved_gate(gate_ref[0], gate_ref[1], index_of, 1)
+
+
+def swap_middle_rows(array):
+    tiles = array.reshape(-1, SUBLANES, LANES)
+    row = sublane_iota((1, SUBLANES, LANES)) >> 1 & 3
+    tiles = jnp.where(
+        row == 1, pltpu.roll(tiles, SUBLANES - 2, 1), jnp.where(row == 2, pltpu.roll(tiles, 2, 1), tiles)
+    )
+    return tiles.reshape(array.shape)
+
+
+def last_gate(gate_ref):
+    def index_of(half, lane):
+        return ((lane >> 1 & 1) << 6) + half * (LANES // 4) + ((lane >> 3) << 1) + (lane & 1)
+
+    return interleaved_gate(swap_middle_rows(gate_ref[0]), swap_middle_rows(gate_ref[1]), index_of, 2)
 
 
 def plan(perm_ref, cycle):
@@ -176,7 +202,7 @@
             store(part, combine(tile_to, at), tiles[at])
 
 
-def local_gates(cycle, load, perm_ref, own_ref, gates, scratch, kept_ref, sent_ref):
+def local_gates(cycle, load, perm_ref, gates, scratch, out_ref, sublane_bit):
     scalars = plan(perm_ref, cycle)
 
     def store(part, tile, value):
@@ -190,79 +216,77 @@
         [out[:, :LANES].reshape(TILES, SUBLANES, LANES), out[:, LANES:].reshape(TILES, SUBLANES, LANES)], axis=0
     )
     tiles = apply_columns(tiles, wide_gate(gates[1, 0], gates[1, 1]))
-    real, imag = gates[2, 0], gates[2, 1]
+    gate = wide_gate(gates[2, 0], gates[2, 1])
     cut = LANES // 2
-    last = jnp.concatenate(
-        [
-            wide_gate(real, imag)[at : at + cut]
-            for at in (0, LANES, cut, LANES + cut)
-        ],
-        axis=0,
-    )
-    out = apply_rows(tiles, last)
-    kept_ref[:, 0] = out[:, :LANES].reshape(TILES, SUBLANES, LANES)
-    kept_ref[:, 1] = out[:, LANES:].reshape(TILES, SUBLANES, LANES)
-    sent_ref[...] = kept_ref[pl.ds((1 - own_ref[0]) * (TILES // 2), TILES // 2)]
-
-
-def first_kernel(perm_ref, own_ref, state_ref, gates_ref, kept_ref, sent_ref, scratch):
+    gate = jnp.concatenate([gate[at : at + cut] for at in (0, LANES, cut, LANES + cut)], axis=0)
+    out = apply_rows(tiles, gate)
+    for bit in range(2):
+        piece = out[:, bit * LANES : (bit + 1) * LANES].reshape(2, TILES // 2, SUBLANES, LANES)
+        out_ref[0, :, bit], out_ref[1, :, bit] = swap_sublane_tile(piece[0], piece[1], sublane_bit)
+
+
+def first_kernel(perm_ref, state_ref, gates_ref, out_ref, scratch):
     def load(part, tile):
         return state_ref[part, :, pl.ds(pl.multiple_of(tile * LANES, LANES), LANES)]
 
-    local_gates(0, load, perm_ref, own_ref, gates_ref.at[0], scratch, kept_ref, sent_ref)
-
-
-def middle_kernel(perm_ref, own_ref, tiles_ref, gates_ref, kept_ref, sent_ref, before, scratch):
-    before[...] = apply_columns(tiles_ref[...], received_gate(gates_ref.at[0, 3])).reshape(before.shape)
+    local_gates(0, load, perm_ref, gates_ref.at[0], scratch, out_ref, 1)
+
+
+def middle_kernel(perm_ref, tiles_ref, gates_ref, out_ref, before, scratch):
+    before[...] = apply_columns(tiles_ref[...], middle_gate(gates_ref.at[0, 3])).reshape(before.shape)
 
     def load(part, tile):
         return before[part, tile]
 
-    local_gates(1, load, perm_ref, own_ref, gates_ref.at[1], scratch, kept_ref, sent_ref)
+    local_gates(1, load, perm_ref, gates_ref.at[1], scratch, out_ref, 2)
 
 
 def last_kernel(tiles_ref, gates_ref, out_ref):
-    tiles = apply_columns(tiles_ref[...], received_gate(gates_ref.at[1, 3])).reshape(2, TILES, SUBLANES, LANES)
-    for tile in range(TILES):
-        out_ref[:, :, tile * LANES : (tile + 1) * LANES] = tiles[:, tile]
+    tiles = swap_sublane_lane(swap_sublane_lane(tiles_ref[...], 0, 5), 2, 6)
+    columns = jnp.concatenate([tiles[:TILES].reshape(WIDE, LANES), tiles[TILES:].reshape(WIDE, LANES)], axis=1)
+    out = product(last_gate(gates_ref.at[1, 3]), columns, ((1,), (0,)))
+    sides = [
+        swap_sublane_lane(out[:, at : at + LANES].reshape(TILES, SUBLANES, LANES), 0, 5) for at in (0, LANES)
+    ]
+    for bit, side in enumerate(swap_sublane_tile(sides[0], sides[1], 1)):
+        side = swap_sublane_lane(side, 2, 6)
+        for at in range(TILES):
+            part, tile = at // (TILES // 2), 2 * (at % (TILES // 2)) + bit
+            out_ref[part, :, tile * LANES : (tile + 1) * LANES] = side[at]
 
 
 SMEM = pl.BlockSpec(memory_space=pltpu.SMEM)
 VMEM = pl.BlockSpec(memory_space=pltpu.VMEM)
 TILE_SHAPE = (2 * TILES, SUBLANES, LANES)
 SCRATCH = pltpu.VMEM((2, TILES, SUBLANES, LANES), jnp.float32)
-TO_SEND = (
-    jax.ShapeDtypeStruct((TILES, 2, SUBLANES, LANES), jnp.float32),
-    jax.ShapeDtypeStruct((TILES // 2, 2, SUBLANES, LANES), jnp.float32),
-)
-
-
-def exchange(kept, sent, own, which):
-    pairs = [(i, i ^ 1 << which) for i in range(lax.axis_size("grp"))]
-    received = lax.ppermute(sent, "grp", pairs)
-    joined = lax.dynamic_update_slice(kept, received, ((1 - own) * (TILES // 2), 0, 0, 0))
-    return lax.all_to_all(joined.reshape(TILE_SHAPE), "dev", split_axis=0, concat_axis=0, tiled=True)
+TO_SEND = jax.ShapeDtypeStruct((2, TILES // 2, 2, SUBLANES, LANES), jnp.float32)
+
+
+def exchange(tiles, axes):
+    ways = 1
+    for axis in axes:
+        ways *= lax.axis_size(axis)
+    chunks = tiles.reshape(ways, -1, LANES)
+    return lax.all_to_all(chunks, axes, split_axis=0, concat_axis=0, tiled=True).reshape(TILE_SHAPE)
 
 
 def on_device(state, gates, local_perm):
-    grp = lax.axis_index("grp")
-    owns = [grp >> cycle & 1 for cycle in range(CYCLES)]
-    kept, sent = pl.pallas_call(
+    tiles = pl.pallas_call(
         first_kernel,
         out_shape=TO_SEND,
-        in_specs=[SMEM, SMEM, VMEM, VMEM],
-        out_specs=(VMEM, VMEM),
+        in_specs=[SMEM, VMEM, VMEM],
+        out_specs=VMEM,
         scratch_shapes=[SCRATCH],
-    )(local_perm, owns[0].reshape(1), state, gates)
-    tiles = exchange(kept, sent, owns[0], 0)
-    kept, sent = pl.pallas_call(
+    )(local_perm, state, gates)
+    tiles = exchange(tiles, ("dev", "grp1", "grp0"))
+    tiles = pl.pallas_call(
         middle_kernel,
         out_shape=TO_SEND,
-        in_specs=[SMEM, SMEM, VMEM, VMEM],
-        out_specs=(VMEM, VMEM),
+        in_specs=[SMEM, VMEM, VMEM],
+        out_specs=VMEM,
         scratch_shapes=[SCRATCH, SCRATCH],
-    )(local_perm, owns[1].reshape(1), tiles, gates)
-    tiles = exchange(kept, sent, owns[1], 1)
+    )(local_perm, tiles, gates)
+    tiles = exchange(tiles, ("dev", "grp1"))
     return pl.pallas_call(
         last_kernel,
         out_shape=jax.ShapeDtypeStruct(state.shape, jnp.float32),
@@ -272,11 +296,13 @@
 
 
 def solution(mesh):
-    placed = (P(None, None, ("grp", "dev")), P(), P())
+    groups, devs = mesh.devices.shape
+    split = Mesh(mesh.devices.reshape(groups // 4, 2, 2, devs), ("grp_rest", "grp1", "grp0", "dev"))
+    placed = P(None, None, ("grp_rest", "grp1", "grp0", "dev"))
     return jax.shard_map(
         on_device,
-        mesh=mesh,
-        in_specs=placed,
-        out_specs=P(None, None, ("grp", "dev")),
+        mesh=split,
+        in_specs=(placed, P(), P()),
+        out_specs=placed,
         check_vma=False,
     )

time: 104 us -> 92.4 us (0.89)
  blocking collectives: 28.6 us -> 79.7 us
  waiting for transfers between devices: 30.9 us -> 0 us
  starting transfers between devices: 30.7 us -> 0 us
  local copies, waits for them, and re-layouts: 2.02 us -> 0 us
    all_to_all x1 -> x2, blocking collectives: 28.6 us -> 79.7 us  [exchange(): lax.all_to_all(chunks, axes, split_axis=0, concat_axis=0, tiled=True)]
    all_to_all x1 -> x0, starting transfers between devices: 22.5 us -> none  [exchange(): lax.all_to_all(joined.reshape(TILE_SHAPE), 'dev', split_axis=0, concat_ax...]
    all_to_all x1 -> x0, waiting for transfers between devices: 22.3 us -> none  [exchange(): lax.all_to_all(joined.reshape(TILE_SHAPE), 'dev', split_axis=0, concat_ax...]
    ppermute x2 -> x0, waiting for transfers between devices: 8.61 us -> none  [exchange(): received = lax.ppermute(sent, 'grp', pairs)]
    ppermute x2 -> x0, starting transfers between devices: 8.21 us -> none  [exchange(): received = lax.ppermute(sent, 'grp', pairs)]
    dynamic_update_slice x2 -> x0, local copies, waits for them, and re-layouts: 1.32 us -> none  [exchange(): lax.dynamic_update_slice(kept, received, ((1 - own) * (TILES // 2), 0, 0,...]
  transfers between devices with their start and end apart: 3 -> 0, of which waited for: 3 -> 0; matrix products, arithmetic and copies ran while one was open for 0% -> 0% of each run, Pallas kernels for 0% -> 0%
where the time goes in v1:
time: 92.4 us; the launch traced here: 91.5 us
  blocking collectives  79.7 us (86%)
  Pallas kernels  11.8 us (13%)
    all_to_all x2, blocking collectives, exchange(): lax.all_to_all(chunks, axes, split_axis=0, concat_axis=0, tiled=True)  79.7 us
    pallas_call x1, Pallas kernels, on_device(): pl.pallas_call(middle_kernel, out_shape=TO_SEND, in_specs=[SMEM, VMEM, VM...  4.85 us
    pallas_call x1, Pallas kernels, on_device(): pl.pallas_call(first_kernel, out_shape=TO_SEND, in_specs=[SMEM, VMEM, VME...  4.07 us
    pallas_call x1, Pallas kernels, on_device(): pl.pallas_call(last_kernel, out_shape=jax.ShapeDtypeStruct(state.shape, j...  2.88 us

profile of v1, /device:TPU:1, one launch (start us, length us, event | category | flops | bytes accessed | tf_op | source)
XLA Modules:
  0.0 91.5 jit_solution(13287565916905115329)
XLA Ops:
  0.0 4.1 %shard_map.37 = f32[2,16,2,8,128]{4,3,2,1,0:T(8,128)} custom-call(s32[2,12]{1,0:T(2,128)} %perm_ref.3, f32[2,8,4096]{2,1,0:T(8,128)} %state_ref.1, f32[2,4,2,128,128]{4,3,2,1,0:T(8,128)} %gates_ref.5), custom_call_target="tpu_custom_call" | custom-call | tf_op jit(solution)/shard_map/pallas_call | solution.py:274
  4.1 51.0 %all_to_all.10 = f32[256,2,128]{2,1,0:T(2,128)} all-to-all(f32[256,2,128]{2,1,0:T(2,128)} %bitcast.7), channel_id=1, replica_groups=mesh['grp_rest'=4,'grp1'=2,'grp0'=2,'dev'=64] {'dev','grp1','grp0'}, dimensions={0} | all-to-all | bytes 524288 | tf_op jit(solution)/shard_map/all_to_all | solution.py:270
  55.1 4.8 %shard_map.38 = f32[2,16,2,8,128]{4,3,2,1,0:T(8,128)} custom-call(s32[2,12]{1,0:T(2,128)} %perm_ref.3, f32[64,8,128]{2,1,0:T(8,128)} %bitcast.4, f32[2,4,2,128,128]{4,3,2,1,0:T(8,128)} %gates_ref.5), custom_call_target="tpu_custom_call" | custom-call | tf_op jit(solution)/shard_map/pallas_call | solution.py:282
  59.9 28.7 %all_to_all.11 = f32[128,4,128]{2,1,0:T(4,128)} all-to-all(f32[128,4,128]{2,1,0:T(4,128)} %bitcast.5), channel_id=1, replica_groups=mesh['grp_rest'=4,'grp1'=2,'grp0'=2,'dev'=64] {'dev','grp1'}, dimensions={0} | all-to-all | bytes 524288 | tf_op jit(solution)/shard_map/all_to_all | solution.py:270
  88.6 2.9 %shard_map.39 = f32[2,8,4096]{2,1,0:T(8,128)} custom-call(f32[64,8,128]{2,1,0:T(8,128)} %bitcast.6, f32[2,4,2,128,128]{4,3,2,1,0:T(8,128)} %gates_ref.5), custom_call_target="tpu_custom_call" | custom-call | tf_op jit(solution)/shard_map/pallas_call | solution.py:290

commit v2 on v1

v2 whole, which is shorter than its diff:
```python
import functools

import jax
import jax.numpy as jnp
from jax import lax
from jax.experimental import pallas as pl
from jax.experimental.pallas import tpu as pltpu
from jax.sharding import Mesh, PartitionSpec as P

CYCLES = 2
LANE_BITS = 7
TILE_BITS = 5
TILES = 1 << TILE_BITS
SUBLANES = 8
LANES = 1 << LANE_BITS
WIDE = 2 * LANES


def lane_iota(shape):
    return lax.broadcasted_iota(jnp.int32, shape, len(shape) - 1)


def sublane_iota(shape):
    return lax.broadcasted_iota(jnp.int32, shape, len(shape) - 2)


def halves(array):
    high = array.astype(jnp.bfloat16)
    return high, (array - high.astype(jnp.float32)).astype(jnp.bfloat16)


def product(left, right, contract):
    left_high, left_low = left
    right_high, right_low = right
    dims = (contract, ((), ()))
    dot = functools.partial(lax.dot_general, dimension_numbers=dims, preferred_element_type=jnp.float32)
    return dot(left_high, right_high) + (dot(left_high, right_low) + dot(left_low, right_high))


def flip_lane_bit(tiles, lane_bit):
    hop = 1 << lane_bit
    if 2 * hop == LANES:
        return pltpu.roll(tiles, hop, 2)
    index = lane_iota((SUBLANES, LANES)) ^ hop
    return jnp.stack([jnp.take_along_axis(tiles[at], index, axis=1) for at in range(tiles.shape[0])])


def swap_sublane_lane(tiles, sublane_bit, lane_bit):
    step = 1 << sublane_bit
    one_tile = (1, SUBLANES, LANES)
    in_sublane = sublane_iota(one_tile) >> sublane_bit & 1
    in_lane = lane_iota(one_tile) >> lane_bit & 1
    if 2 * step == SUBLANES:
        flipped = pltpu.roll(tiles, step, 1)
    else:
        flipped = jnp.where(in_sublane == 0, pltpu.roll(tiles, SUBLANES - step, 1), pltpu.roll(tiles, step, 1))
    return jnp.where(in_sublane == in_lane, tiles, flip_lane_bit(flipped, lane_bit))


def swap_sublane_tile(low, high, sublane_bit):
    step = 1 << sublane_bit
    clear = sublane_iota((1, SUBLANES, LANES)) >> sublane_bit & 1 == 0
    new_low = jnp.where(clear, low, pltpu.roll(high, step, 1))
    new_high = jnp.where(clear, pltpu.roll(low, SUBLANES - step, 1), high)
    return new_low, new_high


def shuffle(tiles):
    tiles = swap_sublane_lane(tiles, 0, 5)
    tiles = swap_sublane_lane(tiles, 1, 6)
    pairs = tiles.reshape(-1, 2, SUBLANES, LANES)
    return jnp.stack(swap_sublane_tile(pairs[:, 0], pairs[:, 1], 2), axis=1).reshape(tiles.shape)


def wide_gate(real, imag):
    return jnp.concatenate(
        [jnp.concatenate([real, -imag], axis=1), jnp.concatenate([imag, real], axis=1)], axis=0
    )


def sending_gate(real, imag):
    gate = wide_gate(real, imag)
    cut = LANES // 2
    return jnp.concatenate([gate[at : at + cut] for at in (0, LANES, cut, LANES + cut)], axis=0)


def take_lanes(array, index):
    rows = [
        jnp.take_along_axis(array[r : r + SUBLANES], index, axis=1) for r in range(0, array.shape[0], SUBLANES)
    ]
    return jnp.concatenate(rows, axis=0)


def apply_rows(tiles, gate):
    parts = tiles.reshape(2, TILES * SUBLANES, LANES)
    return product(halves(jnp.concatenate([parts[0], parts[1]], axis=1)), gate, ((1,), (1,)))


def apply_columns(tiles, gate):
    pairs = shuffle(tiles).reshape(TILES, 2, SUBLANES, LANES)
    columns = jnp.concatenate(
        [pairs[:, 0].reshape(WIDE, LANES), pairs[:, 1].reshape(WIDE, LANES)], axis=1
    )
    out = product(gate, halves(columns), ((1,), (0,)))
    back = jnp.stack(
        [out[:, :LANES].reshape(TILES, SUBLANES, LANES), out[:, LANES:].reshape(TILES, SUBLANES, LANES)], axis=1
    )
    return shuffle(back.reshape(2 * TILES, SUBLANES, LANES))


def interleaved_gate(real, imag, index_of, part_bit):
    lane = lane_iota((SUBLANES, LANES))
    part = lane_iota((1, LANES)) >> part_bit & 1
    blocks = []
    for half in range(2):
        index = index_of(half, lane)
        real_half, imag_half = take_lanes(real, index), take_lanes(imag, index)
        blocks.append(
            jnp.concatenate(
                [jnp.where(part == 0, real_half, -imag_half), jnp.where(part == 0, imag_half, real_half)], axis=0
            )
        )
    return jnp.concatenate(blocks, axis=1)


def middle_gate(gate_ref):
    def index_of(half, lane):
        return half * (LANES // 2) + ((lane >> 2) << 1) + (lane & 1)

    return interleaved_gate(gate_ref[0], gate_ref[1], index_of, 1)


def swap_middle_rows(array):
    tiles = array.reshape(-1, SUBLANES, LANES)
    row = sublane_iota((1, SUBLANES, LANES)) >> 1 & 3
    tiles = jnp.where(
        row == 1, pltpu.roll(tiles, SUBLANES - 2, 1), jnp.where(row == 2, pltpu.roll(tiles, 2, 1), tiles)
    )
    return tiles.reshape(array.shape)


def last_gate(gate_ref):
    def index_of(half, lane):
        return ((lane >> 1 & 1) << 6) + half * (LANES // 4) + ((lane >> 3) << 1) + (lane & 1)

    return interleaved_gate(swap_middle_rows(gate_ref[0]), swap_middle_rows(gate_ref[1]), index_of, 2)


def wire_place(tile):
    z, low = tile >> 2, tile & 3
    return (z & 1) << 5 | (z >> 1 & 1) << 4 | (z >> 2 & 1) << 3 | (z >> 3 & 1) << 2 | low


def arrived_tiles(tiles_ref):
    return jnp.stack([tiles_ref[wire_place(tile)] for tile in range(2 * TILES)])


OUT_OF = 0
CROSSING = OUT_OF + LANE_BITS + TILE_BITS
LANE_OF = CROSSING + TILE_BITS + 1
TABLE = pltpu.SMEM((LANE_OF + LANE_BITS + TILE_BITS,), jnp.int32)


def plan(perm_ref, cycle, table):
    source = [perm_ref[cycle, b] for b in range(LANE_BITS + TILE_BITS)]
    for b in range(LANE_BITS + TILE_BITS):
        table[OUT_OF + source[b]] = jnp.int32(b)
    count = jnp.int32(0)
    for b in range(LANE_BITS, LANE_BITS + TILE_BITS):
        table[CROSSING + count] = jnp.int32(b)
        count = count + jnp.where(source[b] < LANE_BITS, 1, 0)
    for b in range(LANE_BITS):
        table[LANE_OF + b] = jnp.int32(b)
    rank = jnp.int32(0)
    bits = []
    for q in range(TILE_BITS):
        out = table[OUT_OF + LANE_BITS + q]
        crosses = out < LANE_BITS
        partner = table[CROSSING + jnp.where(crosses, rank, 0)]
        rank = rank + jnp.where(crosses, 1, 0)
        origin = perm_ref[cycle, partner]
        table[LANE_OF + LANE_BITS + q] = origin
        target = jnp.where(crosses, partner, out) - LANE_BITS
        bits.append((crosses, out, origin, target))
    lanes = [table[LANE_OF + source[b]] for b in range(LANE_BITS)]
    return bits, lanes


def combine(basis, value):
    total = jnp.int32(0)
    for bit in range(TILE_BITS):
        if value >> bit & 1:
            total = total + basis[bit]
    return total


def permute(load, store, plans):
    bits, lanes = plans
    lane = lane_iota((SUBLANES, LANES))

    def shifted(amount):
        return lax.shift_right_logical(lane, jnp.full((SUBLANES, LANES), amount)) & 1

    never = 31
    before = [shifted(jnp.where(crosses, origin, never)) == 1 for crosses, _, origin, _ in bits]
    after = [shifted(jnp.where(crosses, out, never)) == 1 for crosses, out, _, _ in bits]
    index = jnp.zeros((SUBLANES, LANES), jnp.int32)
    for b in range(LANE_BITS):
        index = index + lax.shift_left(lane >> b & 1, jnp.full((SUBLANES, LANES), lanes[b]))
    flips = [jnp.where(crosses, lax.shift_left(jnp.int32(1), origin), 0) for crosses, _, origin, _ in bits]
    targets = [lax.shift_left(jnp.int32(1), target) for _, _, _, target in bits]

    def trade(tiles, masks):
        for q in range(TILE_BITS):
            for at in range(TILES):
                if not at >> q & 1:
                    low, high = tiles[at], tiles[at + (1 << q)]
                    tiles[at] = jnp.where(masks[q], high, low)
                    tiles[at + (1 << q)] = jnp.where(masks[q], low, high)
        return tiles

    for part in range(2):
        tiles = trade([load(part, at) for at in range(TILES)], before)
        tiles = [
            jnp.take_along_axis(tiles[at], index ^ jnp.full((SUBLANES, LANES), combine(flips, at)), axis=1)
            for at in range(TILES)
        ]
        for at, tile in enumerate(trade(tiles, after)):
            store(part, combine(targets, at), tile)


def local_gates(plans, load, gates, scratch, out_ref, sublane_bit):
    def store(part, tile, value):
        scratch[part, tile] = value

    permute(load, store, plans)
    out = apply_rows(scratch[...].reshape(2 * TILES, SUBLANES, LANES), gates(0))
    tiles = jnp.concatenate(
        [out[:, :LANES].reshape(TILES, SUBLANES, LANES), out[:, LANES:].reshape(TILES, SUBLANES, LANES)], axis=0
    )
    tiles = apply_columns(tiles, gates(1))
    out = apply_rows(tiles, gates(2))
    for bit in range(2):
        piece = out[:, bit * LANES : (bit + 1) * LANES].reshape(2, TILES // 2, SUBLANES, LANES)
        for top, swapped in enumerate(swap_sublane_tile(piece[0], piece[1], sublane_bit)):
            for at in range(TILES // 2):
                out_ref[wire_place(top * TILES + 2 * at + bit)] = swapped[at]


def first_kernel(perm_ref, state_hbm, gates_hbm, out_ref, state_ref, gates_ref, scratch, table, arrived):
    copies = [pltpu.make_async_copy(state_hbm, state_ref, arrived.at[0])]
    for which in range(3):
        copies.append(pltpu.make_async_copy(gates_hbm.at[0, which], gates_ref.at[which], arrived.at[1 + which]))
    for copy in copies:
        copy.start()
    plans = plan(perm_ref, 0, table)
    copies[0].wait()

    def load(part, tile):
        return state_ref[part, :, tile * LANES : (tile + 1) * LANES]

    def gates(which):
        copies[1 + which].wait()
        form = sending_gate if which == 2 else wide_gate
        return halves(form(gates_ref[which, 0], gates_ref[which, 1]))

    local_gates(plans, load, gates, scratch, out_ref, 1)


def gate_kernel(gates_ref, out_ref):
    ready = [
        middle_gate(gates_ref.at[0, 3]),
        wide_gate(gates_ref[1, 0, 0], gates_ref[1, 0, 1]),
        wide_gate(gates_ref[1, 1, 0], gates_ref[1, 1, 1]),
        sending_gate(gates_ref[1, 2, 0], gates_ref[1, 2, 1]),
        last_gate(gates_ref.at[1, 3]),
    ]
    for at, gate in enumerate(ready):
        out_ref[at, 0], out_ref[at, 1] = halves(gate)


def middle_kernel(perm_ref, tiles_ref, gates_ref, out_ref, before, scratch, table):
    plans = plan(perm_ref, 1, table)

    def gates(which):
        return gates_ref[1 + which, 0], gates_ref[1 + which, 1]

    before[...] = apply_columns(arrived_tiles(tiles_ref), gates(-1)).reshape(before.shape)

    def load(part, tile):
        return before[part, tile]

    local_gates(plans, load, gates, scratch, out_ref, 2)


def last_kernel(tiles_ref, gates_ref, out_ref):
    tiles = swap_sublane_lane(swap_sublane_lane(arrived_tiles(tiles_ref), 0, 5), 2, 6)
    columns = jnp.concatenate([tiles[:TILES].reshape(WIDE, LANES), tiles[TILES:].reshape(WIDE, LANES)], axis=1)
    out = product((gates_ref[4, 0], gates_ref[4, 1]), halves(columns), ((1,), (0,)))
    sides = [
        swap_sublane_lane(out[:, at : at + LANES].reshape(TILES, SUBLANES, LANES), 0, 5) for at in (0, LANES)
    ]
    for bit, side in enumerate(swap_sublane_tile(sides[0], sides[1], 1)):
        side = swap_sublane_lane(side, 2, 6)
        for at in range(TILES):
            part, tile = at // (TILES // 2), 2 * (at % (TILES // 2)) + bit
            out_ref[part, :, tile * LANES : (tile + 1) * LANES] = side[at]


SMEM = pl.BlockSpec(memory_space=pltpu.SMEM)
HBM = pl.BlockSpec(memory_space=pltpu.HBM)
VMEM = pl.BlockSpec(memory_space=pltpu.VMEM)
ALL_VMEM = pltpu.CompilerParams(vmem_limit_bytes=67043328)
PARAMS = pltpu.CompilerParams(vmem_limit_bytes=12 << 20)
TILE_SHAPE = (2 * TILES, SUBLANES, LANES)
SCRATCH = pltpu.VMEM((2, TILES, SUBLANES, LANES), jnp.float32)
READY = jax.ShapeDtypeStruct((5, 2, WIDE, WIDE), jnp.bfloat16)
TO_SEND = jax.ShapeDtypeStruct(TILE_SHAPE, jnp.float32)
DEV = ("z0", "z1", "z2", "z3", "dev_low")


def exchange(tiles, axes):
    ways = 1
    for axis in axes:
        ways *= lax.axis_size(axis)
    chunks = tiles.reshape(ways, -1, LANES)
    return lax.all_to_all(chunks, axes, split_axis=0, concat_axis=0, tiled=True).reshape(TILE_SHAPE)


def on_device(state, gates, local_perm):
    tiles = pl.pallas_call(
        first_kernel,
        out_shape=TO_SEND,
        in_specs=[SMEM, HBM, HBM],
        out_specs=VMEM,
        scratch_shapes=[
            pltpu.VMEM(state.shape, jnp.float32),
            pltpu.VMEM((3,) + gates.shape[2:], jnp.float32),
            SCRATCH,
            TABLE,
            pltpu.SemaphoreType.DMA((4,)),
        ],
        compiler_params=ALL_VMEM,
    )(local_perm, state, gates)
    ready = pl.pallas_call(
        gate_kernel,
        out_shape=READY,
        in_specs=[VMEM],
        out_specs=VMEM,
        compiler_params=PARAMS,
        cost_estimate=pl.CostEstimate(flops=10**8, bytes_accessed=4 * 10**6, transcendentals=0),
    )(gates)
    tiles = exchange(tiles, DEV + ("grp1", "grp0"))
    tiles = pl.pallas_call(
        middle_kernel,
        out_shape=TO_SEND,
        in_specs=[SMEM, VMEM, VMEM],
        out_specs=VMEM,
        scratch_shapes=[SCRATCH, SCRATCH, TABLE],
        compiler_params=PARAMS,
    )(local_perm, tiles, ready)
    tiles = exchange(tiles, DEV + ("grp1",))
    return pl.pallas_call(
        last_kernel,
        out_shape=jax.ShapeDtypeStruct(state.shape, jnp.float32),
        in_specs=[VMEM, VMEM],
        out_specs=VMEM,
        compiler_params=PARAMS,
    )(tiles, ready)


def solution(mesh):
    groups, devs = mesh.devices.shape
    names = ("grp_rest", "grp1", "grp0", "z3", "z2", "z1", "z0", "dev_low")
    split = Mesh(mesh.devices.reshape(groups // 4, 2, 2, 2, 2, 2, 2, devs // 16), names)
    placed = P(None, None, names)
    return jax.shard_map(
        on_device,
        mesh=split,
        in_specs=(placed, P(), P()),
        out_specs=placed,
        check_vma=False,
    )
```

time: 92.4 us -> 86.1 us (0.932)
  blocking collectives: 79.7 us -> 29.1 us
  starting transfers between devices: 0 us -> 27.1 us
  waiting for transfers between devices: 0 us -> 19.9 us
  Pallas kernels: 11.8 us -> 8.4 us
  local copies, waits for them, and re-layouts: 0 us -> 1.22 us
    all_to_all x2 -> x1, blocking collectives: 79.7 us -> 29.1 us  [exchange(): lax.all_to_all(chunks, axes, split_axis=0, concat_axis=0, tiled=True)]
    all_to_all x0 -> x1, starting transfers between devices: none -> 27.1 us  [exchange(): lax.all_to_all(chunks, axes, split_axis=0, concat_axis=0, tiled=True)]
    all_to_all x0 -> x1, waiting for transfers between devices: none -> 19.9 us  [exchange(): lax.all_to_all(chunks, axes, split_axis=0, concat_axis=0, tiled=True)]
    pallas_call x1, Pallas kernels: 4.85 us -> 2.71 us  [on_device(): pl.pallas_call(middle_kernel, out_shape=TO_SEND, in_specs=[SMEM, VMEM, VM...]
    pallas_call x1, Pallas kernels: 2.88 us -> 1.3 us  [on_device(): pl.pallas_call(last_kernel, out_shape=jax.ShapeDtypeStruct(state.shape, j...]
    unnamed x0 -> x4, local copies, waits for them, and re-layouts: none -> 1.22 us
    pallas_call x1 -> x2, Pallas kernels: 4.07 us -> 4.4 us  [the longest x1 4.07 us: on_device(): pl.pallas_call(first_kernel, out_shape=TO_SEND, in_specs=[SMEM, HBM, HBM]...]
  transfers between devices with their start and end apart: 0 -> 1, of which waited for: 0 -> 1; matrix products, arithmetic and copies ran while one was open for 0% -> 0% of each run, Pallas kernels for 0% -> 0%
where the time goes in v2:
time: 86.1 us; the launch traced here: 85.8 us
  blocking collectives  29.1 us (34%)
  starting transfers between devices  27.1 us (31%)
  waiting for transfers between devices  19.9 us (23%)
  Pallas kernels  8.4 us (10%)
  local copies, waits for them, and re-layouts  1.22 us (1%)
    all_to_all x1, blocking collectives, exchange(): lax.all_to_all(chunks, axes, split_axis=0, concat_axis=0, tiled=True)  29.1 us
    all_to_all x1, starting transfers between devices, exchange(): lax.all_to_all(chunks, axes, split_axis=0, concat_axis=0, tiled=True)  27.1 us
    all_to_all x1, waiting for transfers between devices, exchange(): lax.all_to_all(chunks, axes, split_axis=0, concat_axis=0, tiled=True)  19.9 us
    pallas_call x1, Pallas kernels, on_device(): pl.pallas_call(first_kernel, out_shape=TO_SEND, in_specs=[SMEM, HBM, HBM]...  4.07 us
    pallas_call x1, Pallas kernels, on_device(): pl.pallas_call(middle_kernel, out_shape=TO_SEND, in_specs=[SMEM, VMEM, VM...  2.71 us
  transfers between devices with their start and end apart: 1, of which 1 were waited for; matrix products, arithmetic and copies ran while one was open for 0% of the time, Pallas kernels for 0%

profile of v2, /device:TPU:1, one launch (start us, length us, event | category | flops | bytes accessed | tf_op | source)
XLA Modules:
  0.0 85.8 jit_solution(12643414041460098477)
XLA Ops:
  0.0 4.1 %shard_map.37 = f32[64,8,128]{2,1,0:T(8,128)} custom-call(s32[2,12]{1,0:T(2,128)} %perm_ref.3, f32[2,8,4096]{2,1,0:T(8,128)} %state_hbm.1, f32[2,4,2,128,128]{4,3,2,1,0:T(8,128)} %gates_ref.1), custom_call_target="tpu_custom_call" | custom-call | tf_op jit(solution)/shard_map/pallas_call | solution.py:331
  4.1 27.1 %all-to-all-start = ((f32[256,2,128]{2,1,0:T(2,128)}), f32[256,2,128]{2,1,0:T(2,128)S(1)}, u32[]{:S(2)}, u32[]{:S(2)}) async-start(f32[256,2,128]{2,1,0:T(2,128)} %bitcast.7), calls=%async_computation | async-start | bytes 524288 | tf_op jit(solution)/shard_map/all_to_all | solution.py:327
  31.2 0.0 copy-start
  31.2 1.2 %copy-done = f32[2,4,2,128,128]{4,3,2,1,0:T(8,128)S(1)} copy-done((f32[2,4,2,128,128]{4,3,2,1,0:T(8,128)S(1)}, f32[2,4,2,128,128]{4,3,2,1,0:T(8,128)}, u32[]{:S(2)}) %copy-start) | copy-done | bytes 1048600
  32.4 0.0 copy-start.1
  32.4 0.3 shard_map.38.gates_ref
  32.7 19.9 %all-to-all-done = f32[256,2,128]{2,1,0:T(2,128)S(1)} async-done(((f32[256,2,128]{2,1,0:T(2,128)}), f32[256,2,128]{2,1,0:T(2,128)S(1)}, u32[]{:S(2)}, u32[]{:S(2)}) %all-to-all-start) | async-done | bytes 262176 | tf_op jit(solution)/shard_map/all_to_all | solution.py:327
  52.6 0.0 copy-done.1
  52.6 2.7 %shard_map.39 = f32[64,8,128]{2,1,0:T(8,128)S(1)} custom-call(s32[2,12]{1,0:T(2,128)S(1)} %copy-done.1, f32[64,8,128]{2,1,0:T(8,128)S(1)} %bitcast.4, bf16[5,2,256,256]{3,2,1,0:T(8,128)(2,1)S(1)} %shard_map.38.gates_ref), custom_call_target="tpu_custom_call" | custom-call | tf_op jit(solution)/shard_map/pallas_call | solution.py:354
  55.3 29.1 %all_to_all.10 = f32[128,4,128]{2,1,0:T(4,128)S(1)} all-to-all(f32[128,4,128]{2,1,0:T(4,128)S(1)} %bitcast.6), channel_id=1, replica_groups=mesh['grp_rest'=4,'grp1'=2,'grp0'=2,'z3'=2,'z2'=2,'z1'=2,'z0'=2,'dev_low..., dimensions={0} | all-to-all | bytes 524288 | tf_op jit(solution)/shard_map/all_to_all | solution.py:327
  84.5 1.3 %shard_map.40 = f32[2,8,4096]{2,1,0:T(8,128)} custom-call(f32[64,8,128]{2,1,0:T(8,128)S(1)} %bitcast.5, bf16[5,2,256,256]{3,2,1,0:T(8,128)(2,1)S(1)} %shard_map.38.gates_ref), custom_call_target="tpu_custom_call" | custom-call | tf_op jit(solution)/shard_map/pallas_call | solution.py:363
Async XLA Ops:
  4.1 48.6 %all-to-all-start = ((f32[256,2,128]{2,1,0:T(2,128)}), f32[256,2,128]{2,1,0:T(2,128)S(1)}, u32[]{:S(2)}, u32[]{:S(2)}) async-start(f32[256,2,128]{2,1,0:T(2,128)} %bitcast.7), calls=%async_computation | async-start | bytes 524288 | tf_op jit(solution)/shard_map/all_to_all | solution.py:327
  31.2 1.2 %copy-start = (f32[2,4,2,128,128]{4,3,2,1,0:T(8,128)S(1)}, f32[2,4,2,128,128]{4,3,2,1,0:T(8,128)}, u32[]{:S(2)}) copy-start(f32[2,4,2,128,128]{4,3,2,1,0:T(8,128)} %gates_ref.1) | copy-start | bytes 3145732
  32.4 20.2 %copy-start.1 = (s32[2,12]{1,0:T(2,128)S(1)}, s32[2,12]{1,0:T(2,128)}, u32[]{:S(2)}) copy-start(s32[2,12]{1,0:T(2,128)} %perm_ref.3) | copy-start | bytes 292

commit v3 on v2

--- a/solution.py
+++ b/solution.py
@@ -14,6 +14,7 @@
 SUBLANES = 8
 LANES = 1 << LANE_BITS
 WIDE = 2 * LANES
+ROW_SPLIT = 2
 
 
 def lane_iota(shape):
@@ -93,7 +94,16 @@
 
 def apply_rows(tiles, gate):
     parts = tiles.reshape(2, TILES * SUBLANES, LANES)
-    return product(halves(jnp.concatenate([parts[0], parts[1]], axis=1)), gate, ((1,), (1,)))
+    rows = TILES * SUBLANES // ROW_SPLIT
+    return jnp.concatenate(
+        [
+            product(
+                halves(jnp.concatenate([parts[0, at : at + rows], parts[1, at : at + rows]], axis=1)), gate, ((1,), (1,))
+            )
+            for at in range(0, TILES * SUBLANES, rows)
+        ],
+        axis=0,
+    )
 
 
 def apply_columns(tiles, gate):
@@ -247,12 +257,15 @@
                 out_ref[wire_place(top * TILES + 2 * at + bit)] = swapped[at]
 
 
-def first_kernel(perm_ref, state_hbm, gates_hbm, out_ref, state_ref, gates_ref, scratch, table, arrived):
+def first_kernel(perm_hbm, state_hbm, gates_hbm, out_ref, perm_ref, state_ref, gates_ref, scratch, table, arrived):
+    perm_copy = pltpu.make_async_copy(perm_hbm, perm_ref, arrived.at[4])
+    perm_copy.start()
     copies = [pltpu.make_async_copy(state_hbm, state_ref, arrived.at[0])]
     for which in range(3):
         copies.append(pltpu.make_async_copy(gates_hbm.at[0, which], gates_ref.at[which], arrived.at[1 + which]))
     for copy in copies:
         copy.start()
+    perm_copy.wait()
     plans = plan(perm_ref, 0, table)
     copies[0].wait()
 
@@ -331,17 +344,18 @@
     tiles = pl.pallas_call(
         first_kernel,
         out_shape=TO_SEND,
-        in_specs=[SMEM, HBM, HBM],
+        in_specs=[HBM, HBM, HBM],
         out_specs=VMEM,
         scratch_shapes=[
+            pltpu.SMEM(local_perm.shape, jnp.int32),
             pltpu.VMEM(state.shape, jnp.float32),
             pltpu.VMEM((3,) + gates.shape[2:], jnp.float32),
             SCRATCH,
             TABLE,
-            pltpu.SemaphoreType.DMA((4,)),
+            pltpu.SemaphoreType.DMA((5,)),
         ],
-        compiler_params=ALL_VMEM,
-    )(local_perm, state, gates)
+        compiler_params=PARAMS,
+    )(*(pltpu.with_memory_space_constraint(array, pltpu.HBM) for array in (local_perm, state, gates)))
     ready = pl.pallas_call(
         gate_kernel,
         out_shape=READY,

time: 86.1 us -> 85.6 us (level)
  local copies, waits for them, and re-layouts: 1.22 us -> 0.01 us
  waiting for transfers between devices: 19.9 us -> 21.1 us
    unnamed x4, local copies, waits for them, and re-layouts: 1.22 us -> 0.01 us
    all_to_all x1, waiting for transfers between devices: 19.9 us -> 21.1 us  [exchange(): lax.all_to_all(chunks, axes, split_axis=0, concat_axis=0, tiled=True)]
where the time goes in v3:
time: 85.6 us; the launch traced here: 85.3 us
  blocking collectives  29.1 us (34%)
  starting transfers between devices  27.1 us (32%)
  waiting for transfers between devices  21.1 us (25%)
  Pallas kernels  7.96 us (9%)
    all_to_all x1, blocking collectives, exchange(): lax.all_to_all(chunks, axes, split_axis=0, concat_axis=0, tiled=True)  29.1 us
    all_to_all x1, starting transfers between devices, exchange(): lax.all_to_all(chunks, axes, split_axis=0, concat_axis=0, tiled=True)  27.1 us
    all_to_all x1, waiting for transfers between devices, exchange(): lax.all_to_all(chunks, axes, split_axis=0, concat_axis=0, tiled=True)  21.1 us
    pallas_call x1, Pallas kernels, on_device(): pl.pallas_call(first_kernel, out_shape=TO_SEND, in_specs=[HBM, HBM, HBM],...  3.6 us
    pallas_call x1, Pallas kernels, on_device(): pl.pallas_call(middle_kernel, out_shape=TO_SEND, in_specs=[SMEM, VMEM, VM...  2.73 us
  transfers between devices with their start and end apart: 1, of which 1 were waited for; matrix products, arithmetic and copies ran while one was open for 0% of the time, Pallas kernels for 0%

profile of v3, /device:TPU:1, one launch (start us, length us, event | category | flops | bytes accessed | tf_op | source)
XLA Modules:
  0.0 85.3 jit_solution(11696731664088465038)
XLA Ops:
  0.0 0.0 copy-start
  0.0 3.6 %shard_map.37 = f32[64,8,128]{2,1,0:T(8,128)} custom-call(s32[2,12]{1,0:T(2,128)} %perm_ref.1, f32[2,8,4096]{2,1,0:T(8,128)} %state_hbm.1, f32[2,4,2,128,128]{4,3,2,1,0:T(8,128)} %gates_ref.1), custom_call_target="tpu_custom_call" | custom-call | tf_op jit(solution)/shard_map/pallas_call | solution.py:344
  3.6 27.1 %all-to-all-start = ((f32[256,2,128]{2,1,0:T(2,128)}), f32[256,2,128]{2,1,0:T(2,128)S(1)}, u32[]{:S(2)}, u32[]{:S(2)}) async-start(f32[256,2,128]{2,1,0:T(2,128)} %bitcast), calls=%async_computation | async-start | bytes 524288 | tf_op jit(solution)/shard_map/all_to_all | solution.py:340
  30.7 0.0 copy-done
  30.7 0.0 copy-start.1
  30.7 0.3 shard_map.38.gates_ref
  31.1 21.1 %all-to-all-done = f32[256,2,128]{2,1,0:T(2,128)S(1)} async-done(((f32[256,2,128]{2,1,0:T(2,128)}), f32[256,2,128]{2,1,0:T(2,128)S(1)}, u32[]{:S(2)}, u32[]{:S(2)}) %all-to-all-start) | async-done | bytes 262176 | tf_op jit(solution)/shard_map/all_to_all | solution.py:340
  52.2 0.0 copy-done.1
  52.2 2.7 %shard_map.39 = f32[64,8,128]{2,1,0:T(8,128)S(1)} custom-call(s32[2,12]{1,0:T(2,128)S(1)} %copy-done.1, f32[64,8,128]{2,1,0:T(8,128)S(1)} %bitcast.4, bf16[5,2,256,256]{3,2,1,0:T(8,128)(2,1)S(1)} %shard_map.38.gates_ref), custom_call_target="tpu_custom_call" | custom-call | tf_op jit(solution)/shard_map/pallas_call | solution.py:368
  54.9 29.1 %all_to_all.10 = f32[128,4,128]{2,1,0:T(4,128)S(1)} all-to-all(f32[128,4,128]{2,1,0:T(4,128)S(1)} %bitcast.6), channel_id=1, replica_groups=mesh['grp_rest'=4,'grp1'=2,'grp0'=2,'z3'=2,'z2'=2,'z1'=2,'z0'=2,'dev_low..., dimensions={0} | all-to-all | bytes 524288 | tf_op jit(solution)/shard_map/all_to_all | solution.py:340
  84.0 1.3 %shard_map.40 = f32[2,8,4096]{2,1,0:T(8,128)} custom-call(f32[64,8,128]{2,1,0:T(8,128)S(1)} %bitcast.5, bf16[5,2,256,256]{3,2,1,0:T(8,128)(2,1)S(1)} %shard_map.38.gates_ref), custom_call_target="tpu_custom_call" | custom-call | tf_op jit(solution)/shard_map/pallas_call | solution.py:377
Async XLA Ops:
  0.0 30.7 %copy-start = (f32[2,4,2,128,128]{4,3,2,1,0:T(8,128)S(1)}, f32[2,4,2,128,128]{4,3,2,1,0:T(8,128)}, u32[]{:S(2)}) copy-start(f32[2,4,2,128,128]{4,3,2,1,0:T(8,128)} %gates_ref.1) | copy-start | bytes 3145732
  3.6 48.6 %all-to-all-start = ((f32[256,2,128]{2,1,0:T(2,128)}), f32[256,2,128]{2,1,0:T(2,128)S(1)}, u32[]{:S(2)}, u32[]{:S(2)}) async-start(f32[256,2,128]{2,1,0:T(2,128)} %bitcast), calls=%async_computation | async-start | bytes 524288 | tf_op jit(solution)/shard_map/all_to_all | solution.py:340
  30.7 21.5 %copy-start.1 = (s32[2,12]{1,0:T(2,128)S(1)}, s32[2,12]{1,0:T(2,128)}, u32[]{:S(2)}) copy-start(s32[2,12]{1,0:T(2,128)} %perm_ref.1) | copy-start | bytes 292

commit v4 on v3

v4 whole, which is shorter than its diff:
```python
import functools

import jax
import jax.numpy as jnp
from jax import lax
from jax.experimental import pallas as pl
from jax.experimental.pallas import tpu as pltpu
from jax.sharding import Mesh, PartitionSpec as P

CYCLES = 2
LANE_BITS = 7
TILE_BITS = 5
TILES = 1 << TILE_BITS
SUBLANES = 8
LANES = 1 << LANE_BITS
WIDE = 2 * LANES


def lane_iota(shape):
    return lax.broadcasted_iota(jnp.int32, shape, len(shape) - 1)


def sublane_iota(shape):
    return lax.broadcasted_iota(jnp.int32, shape, len(shape) - 2)


def halves(array):
    high = array.astype(jnp.bfloat16)
    return high, (array - high.astype(jnp.float32)).astype(jnp.bfloat16)


def product(left, right):
    dims = (((1,), (1,)), ((), ()))
    dot = functools.partial(lax.dot_general, dimension_numbers=dims, preferred_element_type=jnp.float32)
    return dot(left[0], right[0]) + (dot(left[0], right[1]) + dot(left[1], right[0]))


def by_rows(left, right):
    cut = WIDE // 2
    return jnp.concatenate(
        [product(tuple(half[at : at + cut] for half in left), right) for at in (0, cut)], axis=0
    )


def by_columns(left, right):
    cut = WIDE // 2
    return jnp.concatenate(
        [product(left, tuple(half[at : at + cut] for half in right)) for at in (0, cut)], axis=1
    )


def set_lanes(lane_bit):
    return lane_iota((SUBLANES, LANES)) >> lane_bit & 1 == 1


def trade(tiles, masks):
    tiles = list(tiles)
    for tile_bit, mask in masks:
        for at in range(len(tiles)):
            if not at >> tile_bit & 1:
                low, high = tiles[at], tiles[at + (1 << tile_bit)]
                tiles[at] = jnp.where(mask, high, low)
                tiles[at + (1 << tile_bit)] = jnp.where(mask, low, high)
    return tiles


def exchange_tile_lane(tiles, pairs):
    masks = [(tile_bit, set_lanes(lane_bit)) for tile_bit, lane_bit in pairs]
    lane = lane_iota((SUBLANES, LANES))
    tiles = trade(tiles, masks)
    for at in range(len(tiles)):
        hop = sum((at >> tile_bit & 1) << lane_bit for tile_bit, lane_bit in pairs)
        if 2 * hop == LANES:
            tiles[at] = pltpu.roll(tiles[at], hop, 1)
        elif hop:
            tiles[at] = jnp.take_along_axis(tiles[at], lane ^ hop, axis=1)
    return trade(tiles, masks)


def exchange_tile_sublane(tiles, tile_bit, sublane_bit):
    tiles = list(tiles)
    step = 1 << sublane_bit
    clear = sublane_iota((SUBLANES, LANES)) >> sublane_bit & 1 == 0
    for at in range(len(tiles)):
        if not at >> tile_bit & 1:
            low, high = tiles[at], tiles[at + (1 << tile_bit)]
            tiles[at] = jnp.where(clear, low, pltpu.roll(high, step, 0))
            tiles[at + (1 << tile_bit)] = jnp.where(clear, pltpu.roll(low, SUBLANES - step, 0), high)
    return tiles


def tiles_of(array, column):
    return [
        array[at * SUBLANES : (at + 1) * SUBLANES, column * LANES : (column + 1) * LANES] for at in range(TILES)
    ]


def matrix_of(left, right):
    return halves(jnp.concatenate([jnp.concatenate(left, axis=0), jnp.concatenate(right, axis=0)], axis=1))


def wide_gate(real, imag):
    return jnp.concatenate(
        [jnp.concatenate([real, -imag], axis=1), jnp.concatenate([imag, real], axis=1)], axis=0
    )


def sending_gate(real, imag):
    gate = wide_gate(real, imag)
    cut = LANES // 2
    return jnp.concatenate([gate[at : at + cut] for at in (0, LANES, cut, LANES + cut)], axis=0)


def turned(ref):
    return jnp.concatenate([ref[pl.ds(low, LANES // 4, stride=4)] for low in range(4)], axis=0)


def take_lanes(array, index):
    rows = [
        jnp.take_along_axis(array[r : r + SUBLANES], index, axis=1) for r in range(0, array.shape[0], SUBLANES)
    ]
    return jnp.concatenate(rows, axis=0)


def receiving_gate(real, imag):
    lane = lane_iota((SUBLANES, LANES))
    part = lane_iota((1, LANES)) >> LANE_BITS - 1 & 1
    blocks = []
    for half in range(2):
        index = half * (LANES // 2) + ((lane & TILES - 1) << 1) + (lane >> TILE_BITS & 1)
        real_half, imag_half = take_lanes(real, index), take_lanes(imag, index)
        blocks.append(
            jnp.concatenate(
                [jnp.where(part == 0, real_half, -imag_half), jnp.where(part == 0, imag_half, real_half)], axis=0
            )
        )
    return jnp.concatenate(blocks, axis=1)


def wire_place(tile):
    z, low = tile >> 2, tile & 3
    return (z & 1) << 5 | (z >> 1 & 1) << 4 | (z >> 2 & 1) << 3 | (z >> 3 & 1) << 2 | low


def arrived_tiles(tiles_ref):
    return [tiles_ref[wire_place(tile)] for tile in range(2 * TILES)]


OUT_OF = 0
CROSSING = OUT_OF + LANE_BITS + TILE_BITS
LANE_OF = CROSSING + TILE_BITS + 1
TABLE = pltpu.SMEM((LANE_OF + LANE_BITS + TILE_BITS,), jnp.int32)


def plan(source_of, table):
    source = [source_of(b) for b in range(LANE_BITS + TILE_BITS)]
    for b in range(LANE_BITS + TILE_BITS):
        table[OUT_OF + source[b]] = jnp.int32(b)
    count = jnp.int32(0)
    for b in range(LANE_BITS, LANE_BITS + TILE_BITS):
        table[CROSSING + count] = jnp.int32(b)
        count = count + jnp.where(source[b] < LANE_BITS, 1, 0)
    for b in range(LANE_BITS):
        table[LANE_OF + b] = jnp.int32(b)
    rank = jnp.int32(0)
    bits = []
    for q in range(TILE_BITS):
        out = table[OUT_OF + LANE_BITS + q]
        crosses = out < LANE_BITS
        partner = table[CROSSING + jnp.where(crosses, rank, 0)]
        rank = rank + jnp.where(crosses, 1, 0)
        origin = source_of(partner)
        table[LANE_OF + LANE_BITS + q] = origin
        target = jnp.where(crosses, partner, out) - LANE_BITS
        target = jnp.where(target == 0, TILE_BITS - 1, target - 1)
        bits.append((crosses, out, origin, target))
    lanes = [table[LANE_OF + source[b]] for b in range(LANE_BITS)]
    return bits, lanes


def combine(basis, value):
    total = jnp.int32(0)
    for bit in range(TILE_BITS):
        if value >> bit & 1:
            total = total + basis[bit]
    return total


def permute(load, store, plans):
    bits, lanes = plans
    lane = lane_iota((SUBLANES, LANES))

    def shifted(amount):
        return lax.shift_right_logical(lane, jnp.full((SUBLANES, LANES), amount)) & 1

    never = 31
    before = [(q, shifted(jnp.where(bit[0], bit[2], never)) == 1) for q, bit in enumerate(bits)]
    after = [(q, shifted(jnp.where(bit[0], bit[1], never)) == 1) for q, bit in enumerate(bits)]
    index = jnp.zeros((SUBLANES, LANES), jnp.int32)
    for b in range(LANE_BITS):
        index = index + lax.shift_left(lane >> b & 1, jnp.full((SUBLANES, LANES), lanes[b]))
    flips = [jnp.where(crosses, lax.shift_left(jnp.int32(1), origin), 0) for crosses, _, origin, _ in bits]
    targets = [lax.shift_left(jnp.int32(1), target) for _, _, _, target in bits]
    for part in range(2):
        tiles = trade([load(part, at) for at in range(TILES)], before)
        tiles = [
            jnp.take_along_axis(tiles[at], index ^ jnp.full((SUBLANES, LANES), combine(flips, at)), axis=1)
            for at in range(TILES)
        ]
        for at, tile in enumerate(trade(tiles, after)):
            store(part, combine(targets, at), tile)


def local_gates(plans, load, gates, scratch, out_ref, partners, top, last_product):
    def store(part, tile, value):
        scratch[part, tile] = value

    permute(load, store, plans)
    parts = scratch[...].reshape(2, TILES * SUBLANES, LANES)
    out = by_rows(gates(0), halves(jnp.concatenate([parts[0], parts[1]], axis=1)))
    sides = []
    for part in range(2):
        rows = slice(part * (TILES // 2), (part + 1) * (TILES // 2))
        sides.append(exchange_tile_lane(tiles_of(out, 0)[rows] + tiles_of(out, 1)[rows], ((4, 2), (3, 1), (2, 0))))
    out = by_rows(gates(1), matrix_of(*sides))
    sides = []
    for part in range(2):
        rows = slice(part * (TILES // 2), (part + 1) * (TILES // 2))
        sides.append(exchange_tile_lane(tiles_of(out, 0)[rows] + tiles_of(out, 1)[rows], ((3, 6), (2, 5))))
    out = last_product(matrix_of(*sides), gates(2))
    names = ["h3", "h4", "t0", "t1", "t2"]
    for sublane_bit, tile_bit in enumerate(partners):
        names[tile_bit] = ("h0", "h1", "h2")[sublane_bit]
    order = ("h0", "h1", "h2", "h3")
    for low in range(2):
        tiles = tiles_of(out, low)
        for sublane_bit, tile_bit in enumerate(partners):
            tiles = exchange_tile_sublane(tiles, tile_bit, sublane_bit)
        for at, tile in enumerate(tiles):
            device = (at >> top & 1) << 5 | low
            for place, name in enumerate(order):
                device |= (at >> names.index(name) & 1) << place + 1
            out_ref[wire_place(device)] = tile


def first_kernel(perm_hbm, state_hbm, gates_hbm, out_ref, perm_ref, state_ref, gates_ref, scratch, table, arrived):
    perm_copy = pltpu.make_async_copy(perm_hbm, perm_ref, arrived.at[4])
    perm_copy.start()
    copies = [pltpu.make_async_copy(state_hbm, state_ref, arrived.at[0])]
    for which in range(3):
        copies.append(pltpu.make_async_copy(gates_hbm.at[0, which], gates_ref.at[which], arrived.at[1 + which]))
    for copy in copies:
        copy.start()
    perm_copy.wait()
    plans = plan(lambda b: perm_ref[0, b], table)
    copies[0].wait()

    def load(part, tile):
        return state_ref[part, :, tile * LANES : (tile + 1) * LANES]

    def gates(which):
        copies[1 + which].wait()
        if which == 1:
            return halves(wide_gate(turned(gates_ref.at[which, 0]), turned(gates_ref.at[which, 1])))
        form = sending_gate if which == 2 else wide_gate
        return halves(form(gates_ref[which, 0], gates_ref[which, 1]))

    local_gates(plans, load, gates, scratch, out_ref, (2, 1, 4), 3, by_rows)


def gate_kernel(gates_ref, out_ref):
    ready = [
        receiving_gate(gates_ref[0, 3, 0], gates_ref[0, 3, 1]),
        wide_gate(gates_ref[1, 0, 0], gates_ref[1, 0, 1]),
        wide_gate(turned(gates_ref.at[1, 1, 0]), turned(gates_ref.at[1, 1, 1])),
        sending_gate(gates_ref[1, 2, 0], gates_ref[1, 2, 1]),
        receiving_gate(turned(gates_ref.at[1, 3, 0]), turned(gates_ref.at[1, 3, 1])),
    ]
    for at, gate in enumerate(ready):
        out_ref[at, 0], out_ref[at, 1] = halves(gate)


LOW_FIVE = tuple((bit, bit) for bit in range(TILE_BITS))


def middle_kernel(perm_ref, tiles_ref, gates_ref, out_ref, scratch, table):
    def source_of(b):
        source = perm_ref[1, b]
        return jnp.where(source >= TILE_BITS, source - TILE_BITS, source + LANE_BITS)

    plans = plan(source_of, table)

    def gates(which):
        return gates_ref[1 + which, 0], gates_ref[1 + which, 1]

    tiles = arrived_tiles(tiles_ref)
    out = by_columns(
        matrix_of(exchange_tile_lane(tiles[:TILES], LOW_FIVE), exchange_tile_lane(tiles[TILES:], LOW_FIVE)), gates(-1)
    )
    before = (tiles_of(out, 0), tiles_of(out, 1))

    def load(part, tile):
        return before[part][tile]

    local_gates(plans, load, gates, scratch, out_ref, (2, 3, 1), 4, by_columns)


def last_kernel(tiles_ref, gates_ref, out_ref):
    tiles = exchange_tile_sublane(arrived_tiles(tiles_ref), TILE_BITS, 1)
    out = by_columns(
        matrix_of(exchange_tile_lane(tiles[:TILES], LOW_FIVE), exchange_tile_lane(tiles[TILES:], LOW_FIVE)),
        (gates_ref[4, 0], gates_ref[4, 1]),
    )
    for part in range(2):
        for at, tile in enumerate(exchange_tile_lane(tiles_of(out, part), LOW_FIVE)):
            out_ref[part, :, at * LANES : (at + 1) * LANES] = tile


SMEM = pl.BlockSpec(memory_space=pltpu.SMEM)
HBM = pl.BlockSpec(memory_space=pltpu.HBM)
VMEM = pl.BlockSpec(memory_space=pltpu.VMEM)
ALL_VMEM = pltpu.CompilerParams(vmem_limit_bytes=67043328)
PARAMS = pltpu.CompilerParams(vmem_limit_bytes=12 << 20)
TILE_SHAPE = (2 * TILES, SUBLANES, LANES)
SCRATCH = pltpu.VMEM((2, TILES, SUBLANES, LANES), jnp.float32)
READY = jax.ShapeDtypeStruct((5, 2, WIDE, WIDE), jnp.bfloat16)
TO_SEND = jax.ShapeDtypeStruct(TILE_SHAPE, jnp.float32)
DEV = ("z0", "z1", "z2", "z3", "dev_low")


def exchange(tiles, axes):
    ways = 1
    for axis in axes:
        ways *= lax.axis_size(axis)
    chunks = tiles.reshape(ways, -1, LANES)
    return lax.all_to_all(chunks, axes, split_axis=0, concat_axis=0, tiled=True).reshape(TILE_SHAPE)


def on_device(state, gates, local_perm):
    tiles = pl.pallas_call(
        first_kernel,
        out_shape=TO_SEND,
        in_specs=[HBM, HBM, HBM],
        out_specs=VMEM,
        scratch_shapes=[
            pltpu.SMEM(local_perm.shape, jnp.int32),
            pltpu.VMEM(state.shape, jnp.float32),
            pltpu.VMEM((3,) + gates.shape[2:], jnp.float32),
            SCRATCH,
            TABLE,
            pltpu.SemaphoreType.DMA((5,)),
        ],
        compiler_params=PARAMS,
    )(*(pltpu.with_memory_space_constraint(array, pltpu.HBM) for array in (local_perm, state, gates)))
    ready = pl.pallas_call(
        gate_kernel,
        out_shape=READY,
        in_specs=[VMEM],
        out_specs=VMEM,
        compiler_params=PARAMS,
        cost_estimate=pl.CostEstimate(flops=10**8, bytes_accessed=4 * 10**6, transcendentals=0),
    )(gates)
    tiles = exchange(tiles, DEV + ("grp1", "grp0"))
    tiles = pl.pallas_call(
        middle_kernel,
        out_shape=TO_SEND,
        in_specs=[SMEM, VMEM, VMEM],
        out_specs=VMEM,
        scratch_shapes=[SCRATCH, TABLE],
        compiler_params=PARAMS,
    )(local_perm, tiles, ready)
    tiles = exchange(tiles, DEV + ("grp1",))
    return pl.pallas_call(
        last_kernel,
        out_shape=jax.ShapeDtypeStruct(state.shape, jnp.float32),
        in_specs=[VMEM, VMEM],
        out_specs=VMEM,
        compiler_params=PARAMS,
    )(tiles, ready)


def solution(mesh):
    groups, devs = mesh.devices.shape
    names = ("grp_rest", "grp1", "grp0", "z3", "z2", "z1", "z0", "dev_low")
    split = Mesh(mesh.devices.reshape(groups // 4, 2, 2, 2, 2, 2, 2, devs // 16), names)
    placed = P(None, None, names)
    return jax.shard_map(
        on_device,
        mesh=split,
        in_specs=(placed, P(), P()),
        out_specs=placed,
        check_vma=False,
    )
```

time: 85.6 us -> 86 us (level)
  no operation moved by 1% of the time
where the time goes in v4:
time: 86 us; the launch traced here: 85.8 us
  blocking collectives  29.1 us (34%)
  starting transfers between devices  27.1 us (32%)
  waiting for transfers between devices  21.1 us (25%)
  Pallas kernels  8.38 us (10%)
    all_to_all x1, blocking collectives, exchange(): lax.all_to_all(chunks, axes, split_axis=0, concat_axis=0, tiled=True)  29.1 us
    all_to_all x1, starting transfers between devices, exchange(): lax.all_to_all(chunks, axes, split_axis=0, concat_axis=0, tiled=True)  27.1 us
    all_to_all x1, waiting for transfers between devices, exchange(): lax.all_to_all(chunks, axes, split_axis=0, concat_axis=0, tiled=True)  21.1 us
    pallas_call x1, Pallas kernels, on_device(): pl.pallas_call(first_kernel, out_shape=TO_SEND, in_specs=[HBM, HBM, HBM],...  3.62 us
    pallas_call x1, Pallas kernels, on_device(): pl.pallas_call(middle_kernel, out_shape=TO_SEND, in_specs=[SMEM, VMEM, VM...  2.85 us
  transfers between devices with their start and end apart: 1, of which 1 were waited for; matrix products, arithmetic and copies ran while one was open for 0% of the time, Pallas kernels for 0%

profile of v4, /device:TPU:1, one launch (start us, length us, event | category | flops | bytes accessed | tf_op | source)
XLA Modules:
  0.0 85.8 jit_solution(4781765196817563674)
XLA Ops:
  0.0 0.0 copy-start
  0.0 3.6 %shard_map.37 = f32[64,8,128]{2,1,0:T(8,128)} custom-call(s32[2,12]{1,0:T(2,128)} %perm_ref.1, f32[2,8,4096]{2,1,0:T(8,128)} %state_hbm.1, f32[2,4,2,128,128]{4,3,2,1,0:T(8,128)} %gates_ref.1), custom_call_target="tpu_custom_call" | custom-call | tf_op jit(solution)/shard_map/pallas_call | solution.py:340
  3.6 27.1 %all-to-all-start = ((f32[256,2,128]{2,1,0:T(2,128)}), f32[256,2,128]{2,1,0:T(2,128)S(1)}, u32[]{:S(2)}, u32[]{:S(2)}) async-start(f32[256,2,128]{2,1,0:T(2,128)} %bitcast), calls=%async_computation | async-start | bytes 524288 | tf_op jit(solution)/shard_map/all_to_all | solution.py:336
  30.7 0.0 copy-done
  30.7 0.0 copy-start.1
  30.8 0.3 shard_map.38.gates_ref
  31.1 21.1 %all-to-all-done = f32[256,2,128]{2,1,0:T(2,128)S(1)} async-done(((f32[256,2,128]{2,1,0:T(2,128)}), f32[256,2,128]{2,1,0:T(2,128)S(1)}, u32[]{:S(2)}, u32[]{:S(2)}) %all-to-all-start) | async-done | bytes 262176 | tf_op jit(solution)/shard_map/all_to_all | solution.py:336
  52.2 0.0 copy-done.1
  52.2 2.8 %shard_map.39 = f32[64,8,128]{2,1,0:T(8,128)S(1)} custom-call(s32[2,12]{1,0:T(2,128)S(1)} %copy-done.1, f32[64,8,128]{2,1,0:T(8,128)S(1)} %bitcast.4, bf16[5,2,256,256]{3,2,1,0:T(8,128)(2,1)S(1)} %shard_map.38.gates_ref), custom_call_target="tpu_custom_call" | custom-call | tf_op jit(solution)/shard_map/pallas_call | solution.py:364
  55.1 29.1 %all_to_all.10 = f32[128,4,128]{2,1,0:T(4,128)S(1)} all-to-all(f32[128,4,128]{2,1,0:T(4,128)S(1)} %bitcast.6), channel_id=1, replica_groups=mesh['grp_rest'=4,'grp1'=2,'grp0'=2,'z3'=2,'z2'=2,'z1'=2,'z0'=2,'dev_low..., dimensions={0} | all-to-all | bytes 524288 | tf_op jit(solution)/shard_map/all_to_all | solution.py:336
  84.2 1.6 %shard_map.40 = f32[2,8,4096]{2,1,0:T(8,128)} custom-call(f32[64,8,128]{2,1,0:T(8,128)S(1)} %bitcast.5, bf16[5,2,256,256]{3,2,1,0:T(8,128)(2,1)S(1)} %shard_map.38.gates_ref), custom_call_target="tpu_custom_call" | custom-call | tf_op jit(solution)/shard_map/pallas_call | solution.py:373
Async XLA Ops:
  0.0 30.7 %copy-start = (f32[2,4,2,128,128]{4,3,2,1,0:T(8,128)S(1)}, f32[2,4,2,128,128]{4,3,2,1,0:T(8,128)}, u32[]{:S(2)}) copy-start(f32[2,4,2,128,128]{4,3,2,1,0:T(8,128)} %gates_ref.1) | copy-start | bytes 3145732
  3.6 48.6 %all-to-all-start = ((f32[256,2,128]{2,1,0:T(2,128)}), f32[256,2,128]{2,1,0:T(2,128)S(1)}, u32[]{:S(2)}, u32[]{:S(2)}) async-start(f32[256,2,128]{2,1,0:T(2,128)} %bitcast), calls=%async_computation | async-start | bytes 524288 | tf_op jit(solution)/shard_map/all_to_all | solution.py:336
  30.7 21.5 %copy-start.1 = (s32[2,12]{1,0:T(2,128)S(1)}, s32[2,12]{1,0:T(2,128)}, u32[]{:S(2)}) copy-start(s32[2,12]{1,0:T(2,128)} %perm_ref.1) | copy-start | bytes 292

commit v5 on v4

--- a/solution.py
+++ b/solution.py
@@ -29,8 +29,8 @@
     return high, (array - high.astype(jnp.float32)).astype(jnp.bfloat16)
 
 
-def product(left, right):
-    dims = (((1,), (1,)), ((), ()))
+def product(left, right, right_axis=1):
+    dims = (((1,), (right_axis,)), ((), ()))
     dot = functools.partial(lax.dot_general, dimension_numbers=dims, preferred_element_type=jnp.float32)
     return dot(left[0], right[0]) + (dot(left[0], right[1]) + dot(left[1], right[0]))
 
@@ -99,6 +99,43 @@
     return halves(jnp.concatenate([jnp.concatenate(left, axis=0), jnp.concatenate(right, axis=0)], axis=1))
 
 
+def flip_lane_bit(tiles, lane_bit):
+    hop = 1 << lane_bit
+    if 2 * hop == LANES:
+        return pltpu.roll(tiles, hop, 2)
+    index = lane_iota((SUBLANES, LANES)) ^ hop
+    return jnp.stack([jnp.take_along_axis(tiles[at], index, axis=1) for at in range(tiles.shape[0])])
+
+
+def swap_sublane_lane(tiles, sublane_bit, lane_bit):
+    step = 1 << sublane_bit
+    one_tile = (1, SUBLANES, LANES)
+    in_sublane = sublane_iota(one_tile) >> sublane_bit & 1
+    in_lane = lane_iota(one_tile) >> lane_bit & 1
+    if 2 * step == SUBLANES:
+        flipped = pltpu.roll(tiles, step, 1)
+    else:
+        flipped = jnp.where(in_sublane == 0, pltpu.roll(tiles, SUBLANES - step, 1), pltpu.roll(tiles, step, 1))
+    return jnp.where(in_sublane == in_lane, tiles, flip_lane_bit(flipped, lane_bit))
+
+
+def swap_sublane_tile(low, high, sublane_bit):
+    step = 1 << sublane_bit
+    clear = sublane_iota((1, SUBLANES, LANES)) >> sublane_bit & 1 == 0
+    new_low = jnp.where(clear, low, pltpu.roll(high, step, 1))
+    new_high = jnp.where(clear, pltpu.roll(low, SUBLANES - step, 1), high)
+    return new_low, new_high
+
+
+def swap_middle_rows(array):
+    tiles = array.reshape(-1, SUBLANES, LANES)
+    row = sublane_iota((1, SUBLANES, LANES)) >> 1 & 3
+    tiles = jnp.where(
+        row == 1, pltpu.roll(tiles, SUBLANES - 2, 1), jnp.where(row == 2, pltpu.roll(tiles, 2, 1), tiles)
+    )
+    return tiles.reshape(array.shape)
+
+
 def wide_gate(real, imag):
     return jnp.concatenate(
         [jnp.concatenate([real, -imag], axis=1), jnp.concatenate([imag, real], axis=1)], axis=0
@@ -128,6 +165,22 @@
     blocks = []
     for half in range(2):
         index = half * (LANES // 2) + ((lane & TILES - 1) << 1) + (lane >> TILE_BITS & 1)
+        real_half, imag_half = take_lanes(real, index), take_lanes(imag, index)
+        blocks.append(
+            jnp.concatenate(
+                [jnp.where(part == 0, real_half, -imag_half), jnp.where(part == 0, imag_half, real_half)], axis=0
+            )
+        )
+    return jnp.concatenate(blocks, axis=1)
+
+
+def last_gate(real, imag):
+    real, imag = swap_middle_rows(real), swap_middle_rows(imag)
+    lane = lane_iota((SUBLANES, LANES))
+    part = lane_iota((1, LANES)) >> 2 & 1
+    blocks = []
+    for half in range(2):
+        index = ((lane >> 1 & 1) << 6) + half * (LANES // 4) + ((lane >> 3) << 1) + (lane & 1)
         real_half, imag_half = take_lanes(real, index), take_lanes(imag, index)
         blocks.append(
             jnp.concatenate(
@@ -217,12 +270,12 @@
 
     permute(load, store, plans)
     parts = scratch[...].reshape(2, TILES * SUBLANES, LANES)
-    out = by_rows(gates(0), halves(jnp.concatenate([parts[0], parts[1]], axis=1)))
+    out = product(gates(0), halves(jnp.concatenate([parts[0], parts[1]], axis=1)))
     sides = []
     for part in range(2):
         rows = slice(part * (TILES // 2), (part + 1) * (TILES // 2))
         sides.append(exchange_tile_lane(tiles_of(out, 0)[rows] + tiles_of(out, 1)[rows], ((4, 2), (3, 1), (2, 0))))
-    out = by_rows(gates(1), matrix_of(*sides))
+    out = product(gates(1), matrix_of(*sides))
     sides = []
     for part in range(2):
         rows = slice(part * (TILES // 2), (part + 1) * (TILES // 2))
@@ -265,16 +318,19 @@
         form = sending_gate if which == 2 else wide_gate
         return halves(form(gates_ref[which, 0], gates_ref[which, 1]))
 
-    local_gates(plans, load, gates, scratch, out_ref, (2, 1, 4), 3, by_rows)
-
-
-def gate_kernel(gates_ref, out_ref):
+    local_gates(plans, load, gates, scratch, out_ref, (2, 1, 4), 3, product)
+
+
+def gate_kernel(gates_hbm, out_ref, gates_ref, arrived):
+    copy = pltpu.make_async_copy(gates_hbm, gates_ref, arrived)
+    copy.start()
+    copy.wait()
     ready = [
         receiving_gate(gates_ref[0, 3, 0], gates_ref[0, 3, 1]),
         wide_gate(gates_ref[1, 0, 0], gates_ref[1, 0, 1]),
         wide_gate(turned(gates_ref.at[1, 1, 0]), turned(gates_ref.at[1, 1, 1])),
         sending_gate(gates_ref[1, 2, 0], gates_ref[1, 2, 1]),
-        receiving_gate(turned(gates_ref.at[1, 3, 0]), turned(gates_ref.at[1, 3, 1])),
+        last_gate(gates_ref[1, 3, 0], gates_ref[1, 3, 1]),
     ]
     for at, gate in enumerate(ready):
         out_ref[at, 0], out_ref[at, 1] = halves(gate)
@@ -294,7 +350,7 @@
         return gates_ref[1 + which, 0], gates_ref[1 + which, 1]
 
     tiles = arrived_tiles(tiles_ref)
-    out = by_columns(
+    out = product(
         matrix_of(exchange_tile_lane(tiles[:TILES], LOW_FIVE), exchange_tile_lane(tiles[TILES:], LOW_FIVE)), gates(-1)
     )
     before = (tiles_of(out, 0), tiles_of(out, 1))
@@ -302,18 +358,21 @@
     def load(part, tile):
         return before[part][tile]
 
-    local_gates(plans, load, gates, scratch, out_ref, (2, 3, 1), 4, by_columns)
+    local_gates(plans, load, gates, scratch, out_ref, (2, 3, 1), 4, product)
 
 
 def last_kernel(tiles_ref, gates_ref, out_ref):
-    tiles = exchange_tile_sublane(arrived_tiles(tiles_ref), TILE_BITS, 1)
-    out = by_columns(
-        matrix_of(exchange_tile_lane(tiles[:TILES], LOW_FIVE), exchange_tile_lane(tiles[TILES:], LOW_FIVE)),
-        (gates_ref[4, 0], gates_ref[4, 1]),
-    )
-    for part in range(2):
-        for at, tile in enumerate(exchange_tile_lane(tiles_of(out, part), LOW_FIVE)):
-            out_ref[part, :, at * LANES : (at + 1) * LANES] = tile
+    tiles = swap_sublane_lane(swap_sublane_lane(jnp.stack(arrived_tiles(tiles_ref)), 0, 5), 2, 6)
+    columns = jnp.concatenate([tiles[:TILES].reshape(WIDE, LANES), tiles[TILES:].reshape(WIDE, LANES)], axis=1)
+    out = product((gates_ref[4, 0], gates_ref[4, 1]), halves(columns), 0)
+    sides = [
+        swap_sublane_lane(out[:, at : at + LANES].reshape(TILES, SUBLANES, LANES), 0, 5) for at in (0, LANES)
+    ]
+    for bit, side in enumerate(swap_sublane_tile(sides[0], sides[1], 1)):
+        side = swap_sublane_lane(side, 2, 6)
+        for at in range(TILES):
+            part, tile = at // (TILES // 2), 2 * (at % (TILES // 2)) + bit
+            out_ref[part, :, tile * LANES : (tile + 1) * LANES] = side[at]
 
 
 SMEM = pl.BlockSpec(memory_space=pltpu.SMEM)
@@ -355,11 +414,12 @@
     ready = pl.pallas_call(
         gate_kernel,
         out_shape=READY,
-        in_specs=[VMEM],
+        in_specs=[HBM],
         out_specs=VMEM,
+        scratch_shapes=[pltpu.VMEM(gates.shape, jnp.float32), pltpu.SemaphoreType.DMA],
         compiler_params=PARAMS,
         cost_estimate=pl.CostEstimate(flops=10**8, bytes_accessed=4 * 10**6, transcendentals=0),
-    )(gates)
+    )(pltpu.with_memory_space_constraint(gates, pltpu.HBM))
     tiles = exchange(tiles, DEV + ("grp1", "grp0"))
     tiles = pl.pallas_call(
         middle_kernel,

time: 86 us -> 85.4 us (level)
  waiting for transfers between devices: 21.1 us -> 19.9 us
    pallas_call x1, Pallas kernels: 0.34 us -> 1.6 us  [on_device(): pl.pallas_call(gate_kernel, out_shape=READY, in_specs=[HBM], out_specs=VM...]
    all_to_all x1, waiting for transfers between devices: 21.1 us -> 19.9 us  [exchange(): lax.all_to_all(chunks, axes, split_axis=0, concat_axis=0, tiled=True)]
  transfers between devices with their start and end apart: 1 -> 1, of which waited for: 1 -> 1; matrix products, arithmetic and copies ran while one was open for 0% -> 0% of each run, Pallas kernels for 0% -> 2%
where the time goes in v5:
time: 85.4 us; the launch traced here: 85.1 us
  blocking collectives  29.1 us (34%)
  starting transfers between devices  27.1 us (32%)
  waiting for transfers between devices  19.9 us (23%)
  Pallas kernels  9.03 us (11%)
    all_to_all x1, blocking collectives, exchange(): lax.all_to_all(chunks, axes, split_axis=0, concat_axis=0, tiled=True)  29.1 us
    all_to_all x1, starting transfers between devices, exchange(): lax.all_to_all(chunks, axes, split_axis=0, concat_axis=0, tiled=True)  27.1 us
    all_to_all x1, waiting for transfers between devices, exchange(): lax.all_to_all(chunks, axes, split_axis=0, concat_axis=0, tiled=True)  19.9 us
    pallas_call x1, Pallas kernels, on_device(): pl.pallas_call(first_kernel, out_shape=TO_SEND, in_specs=[HBM, HBM, HBM],...  3.38 us
    pallas_call x1, Pallas kernels, on_device(): pl.pallas_call(middle_kernel, out_shape=TO_SEND, in_specs=[SMEM, VMEM, VM...  2.76 us
  transfers between devices with their start and end apart: 1, of which 1 were waited for; matrix products, arithmetic and copies ran while one was open for 0% of the time, Pallas kernels for 2%

profile of v5, /device:TPU:1, one launch (start us, length us, event | category | flops | bytes accessed | tf_op | source)
XLA Modules:
  0.0 85.1 jit_solution(2188574333593378085)
XLA Ops:
  0.0 3.4 %shard_map.37 = f32[64,8,128]{2,1,0:T(8,128)} custom-call(s32[2,12]{1,0:T(2,128)} %perm_ref.1, f32[2,8,4096]{2,1,0:T(8,128)} %state_hbm.1, f32[2,4,2,128,128]{4,3,2,1,0:T(8,128)} %gates_hbm.3), custom_call_target="tpu_custom_call" | custom-call | tf_op jit(solution)/shard_map/pallas_call | solution.py:399
  3.4 27.1 %all-to-all-start = ((f32[256,2,128]{2,1,0:T(2,128)}), f32[256,2,128]{2,1,0:T(2,128)S(1)}, u32[]{:S(2)}, u32[]{:S(2)}) async-start(f32[256,2,128]{2,1,0:T(2,128)} %bitcast), calls=%async_computation | async-start | bytes 524288 | tf_op jit(solution)/shard_map/all_to_all | solution.py:395
  30.5 0.0 copy-start
  30.5 1.6 %shard_map.38.gates_ref = bf16[5,2,256,256]{3,2,1,0:T(8,128)(2,1)S(1)} custom-call(f32[2,4,2,128,128]{4,3,2,1,0:T(8,128)} %gates_hbm.3), custom_call_target="tpu_custom_call" | custom-call | flops 100000000 | bytes 4000000 | tf_op jit(solution)/shard_map/pallas_call | solution.py:414
  32.1 19.9 %all-to-all-done = f32[256,2,128]{2,1,0:T(2,128)S(1)} async-done(((f32[256,2,128]{2,1,0:T(2,128)}), f32[256,2,128]{2,1,0:T(2,128)S(1)}, u32[]{:S(2)}, u32[]{:S(2)}) %all-to-all-start) | async-done | bytes 262176 | tf_op jit(solution)/shard_map/all_to_all | solution.py:395
  51.9 0.0 copy-done
  51.9 2.8 %shard_map.39 = f32[64,8,128]{2,1,0:T(8,128)S(1)} custom-call(s32[2,12]{1,0:T(2,128)S(1)} %copy-done, f32[64,8,128]{2,1,0:T(8,128)S(1)} %bitcast.4, bf16[5,2,256,256]{3,2,1,0:T(8,128)(2,1)S(1)} %shard_map.38.gates_ref), custom_call_target="tpu_custom_call" | custom-call | tf_op jit(solution)/shard_map/pallas_call | solution.py:424
  54.7 29.1 %all_to_all.10 = f32[128,4,128]{2,1,0:T(4,128)S(1)} all-to-all(f32[128,4,128]{2,1,0:T(4,128)S(1)} %bitcast.6), channel_id=1, replica_groups=mesh['grp_rest'=4,'grp1'=2,'grp0'=2,'z3'=2,'z2'=2,'z1'=2,'z0'=2,'dev_low..., dimensions={0} | all-to-all | bytes 524288 | tf_op jit(solution)/shard_map/all_to_all | solution.py:395
  83.8 1.3 %shard_map.40 = f32[2,8,4096]{2,1,0:T(8,128)} custom-call(f32[64,8,128]{2,1,0:T(8,128)S(1)} %bitcast.5, bf16[5,2,256,256]{3,2,1,0:T(8,128)(2,1)S(1)} %shard_map.38.gates_ref), custom_call_target="tpu_custom_call" | custom-call | tf_op jit(solution)/shard_map/pallas_call | solution.py:433
Async XLA Ops:
  3.4 48.6 %all-to-all-start = ((f32[256,2,128]{2,1,0:T(2,128)}), f32[256,2,128]{2,1,0:T(2,128)S(1)}, u32[]{:S(2)}, u32[]{:S(2)}) async-start(f32[256,2,128]{2,1,0:T(2,128)} %bitcast), calls=%async_computation | async-start | bytes 524288 | tf_op jit(solution)/shard_map/all_to_all | solution.py:395
  30.5 21.5 %copy-start = (s32[2,12]{1,0:T(2,128)S(1)}, s32[2,12]{1,0:T(2,128)}, u32[]{:S(2)}) copy-start(s32[2,12]{1,0:T(2,128)} %perm_ref.1) | copy-start | bytes 292
